TPU v7x, 32 devices: a whole 2x2x4 slice. The times are simulated.
32 devices in a mesh: grp: 4 (over z), tile: 2 (over y), arch: 4 (over x, core).
Axes of the slice: x: 2, y: 2, z: 4, core: 2. Of those that a mesh axis runs over, the one named last changes fastest.
Arguments:
- query_grads: bfloat16 [4, 1536, 4096], P('arch', 'tile', 'grp'), may hold values from -6 to 6
- input_basis: bfloat16 [4096, 4096], P(None, 'grp'), may hold values from -0.09375 to 0.09375
- output_basis: bfloat16 [1536, 1536], P(None, 'tile'), may hold values from -0.15625 to 0.15625
- eigenvalues: float32 [1536, 4096], P('tile', 'grp'), may hold values from 0.1 to 10
- activations: bfloat16 [1024, 4096], P('arch', 'grp'), may hold values from -6 to 6
- gradients: bfloat16 [1024, 1536], P('arch', 'tile'), may hold values from -0.0099487305 to 0.0099487305
- seq_lengths: int32 [4, 8], P('arch'), may hold values from 1 to 128, 256 in all within a row
Outputs:
- preconditioned: bfloat16 [4, 4096, 1536], P('arch', 'grp', 'tile')
- sequence_scores: float32 [4, 32], P(None, 'arch')
Inputs may be any that keep to these rules, and one draw needn't show every extreme that they name: Each row of seq_lengths sums to 256, and its largest entry is exactly 128.
All inputs are finite; a program needn't handle non-finite values.
Results may differ from a plain program's by a relative error of at most 0.013.
Values may be sent and summed in bfloat16 or wider, within the bound.
No kernel may reach another device: no remote copies, remote signals or barrier semaphores. Data moves between devices by JAX's collectives and lax.ppermute only.
A program may use at most 64 MiB of HBM per device.

v0:
```python
import jax
import jax.numpy as jnp
from jax import lax
from jax.sharding import PartitionSpec as P

damping = 0.01


def contract_first(left_side, right_side):
    return lax.dot_general(
        left_side, right_side, (((0,), (0,)), ((), ())), preferred_element_type=jnp.float32
    )


def contract_last(left_side, right_side):
    return lax.dot_general(
        left_side, right_side, (((1,), (1,)), ((), ())), preferred_element_type=jnp.float32
    )


def per_device(
    query_grads, input_basis, output_basis, eigenvalues, activations, gradients, seq_lengths
):
    local_query = query_grads[0]
    feat_rows = local_query.shape[0]
    input_cols = local_query.shape[1]
    basis_part = input_basis
    rotated_in = jnp.dot(
        lax.all_gather(local_query, "grp", axis=1, tiled=True),
        basis_part,
        preferred_element_type=jnp.float32,
    ).astype(jnp.bfloat16)
    basis_part = output_basis
    rotated = contract_first(basis_part, lax.all_gather(rotated_in, "tile", axis=0, tiled=True))
    scaled = (rotated / (eigenvalues + damping)).astype(jnp.bfloat16)
    basis_part = output_basis
    restored = lax.psum_scatter(
        jnp.dot(basis_part, scaled, preferred_element_type=jnp.float32).astype(jnp.bfloat16),
        "tile",
        scatter_dimension=0,
        tiled=True,
    )
    basis_part = input_basis
    summed = lax.psum_scatter(
        contract_last(basis_part, restored), "grp", scatter_dimension=0, tiled=True
    )
    preconditioned = summed.astype(jnp.bfloat16)
    all_queries = lax.all_gather(preconditioned[None], "arch", axis=0, tiled=True)
    query_count = all_queries.shape[0]
    stacked = jnp.transpose(all_queries, (1, 0, 2)).reshape(input_cols, query_count * feat_rows)
    projected = jnp.dot(activations, stacked, preferred_element_type=jnp.float32)
    projected = projected.reshape(activations.shape[0], query_count, feat_rows)
    partial_scores = jnp.sum(projected * gradients.astype(jnp.float32)[:, None, :], axis=2).T
    lengths = seq_lengths[0]
    ends = jnp.cumsum(lengths)
    starts = ends - lengths
    position = jnp.arange(activations.shape[0], dtype=jnp.int32)
    member = ((position[None, :] >= starts[:, None]) & (position[None, :] < ends[:, None])).astype(
        jnp.float32
    )
    seq_sizes = lengths.astype(jnp.float32)
    partial_totals = jnp.dot(partial_scores, member.T, precision=lax.Precision.HIGHEST)
    totals = lax.psum(partial_totals, ("grp", "tile"))
    sequence_scores = totals / seq_sizes[None, :]
    return (preconditioned[None], sequence_scores)


def solution(mesh):
    return jax.shard_map(
        per_device,
        mesh=mesh,
        in_specs=(
            P("arch", "tile", "grp"),
            P(None, "grp"),
            P(None, "tile"),
            P("tile", "grp"),
            P("arch", "grp"),
            P("arch", "tile"),
            P("arch", None),
        ),
        out_specs=(P("arch", "grp", "tile"), P(None, "arch")),
        check_vma=False,
    )
```

profile of v0, /device:TPU:0, one launch (start us, length us, event | category | flops | bytes accessed | tf_op | source)
XLA Modules:
  0.0 545.8 jit_solution(10824075178936994615)
XLA Ops:
  7.2 0.0 copy-start
  7.2 0.0 all-gather.8.cloned.1.call-start
  7.2 0.7 all-gather.8.cloned.1.call-update
  7.9 0.0 all-gather.6.cloned.1.call-start
  8.0 119.7 %all-gather.8.cloned.1.call-done = bf16[1,768,4096]{2,1,0:T(8,128)(2,1)} async-done(((bf16[1,768,1024]{2,1,0:T(8,128)(2,1)}), bf16[1,768,4096]{2,1,0:T(8,128)(2,1)}) %all-gather.8.cloned.1.call-update) | async-done | bytes 6291472 | tf_op jit(solution)/shard_map/all_gather | solution.py:29
  127.6 12.0 %fusion.4 = bf16[768,1024]{1,0:T(8,128)(2,1)} fusion(bf16[4096,1024]{1,0:T(8,128)(2,1)} %param.8, bf16[1,768,4096]{2,1,0:T(8,128)(2,1)} %all-gather.8.cloned.1.call-done), kind=kOutput, calls=%fused_computation.9 | convolution fusion | flops 6443237376 | bytes 16252928 | tf_op jit(solution)/shard_map/dot_general | solution.py:28
  139.7 0.0 all-gather.6.cloned.1.call-update
  139.7 0.0 reduce-scatter.3.cloned.1.call-start
  139.8 3.6 copy.14
  143.4 39.6 %all-gather.6.cloned.1.call-done = bf16[1536,1024]{1,0:T(8,128)(2,1)} async-done(((bf16[768,1024]{1,0:T(8,128)(2,1)}), bf16[1536,1024]{1,0:T(8,128)(2,1)}) %all-gather.6.cloned.1.call-update) | async-done | bytes 3145744 | tf_op jit(solution)/shard_map/all_gather | solution.py:34
  183.0 0.0 copy-done
  183.0 9.7 %fusion.2 = bf16[1536,1024]{0,1:T(8,128)(2,1)} fusion(bf16[1536,768]{1,0:T(8,128)(2,1)S(1)} %copy-done, f32[768,1024]{0,1:T(8,128)} %copy.14, bf16[1536,1024]{1,0:T(8,128)(2,1)} %all-gather.6.cloned.1.call-done), kind=kOutput, calls=%fused_computation.5 | convolution fusion | flops 4835770368 | bytes 11796480 | tf_op jit(solution)/shard_map/dot_general | solution.py:38
  192.6 0.0 reduce-scatter.3.cloned.1.call-update
  192.6 0.0 reduce-scatter.5.cloned.1.call-start
  192.7 43.5 %reduce-scatter.3.cloned.1.call-done = bf16[768,1024]{0,1:T(8,128)(2,1)} async-done(((bf16[1536,1024]{0,1:T(8,128)(2,1)}), bf16[768,1024]{0,1:T(8,128)(2,1)}) %reduce-scatter.3.cloned.1.call-update) | async-done | bytes 1572880 | tf_op jit(solution)/shard_map/reduce_scatter | solution.py:37
  236.2 12.2 %convolution_bitcast_fusion = f32[4096,768]{0,1:T(8,128)} fusion(bf16[768,1024]{0,1:T(8,128)(2,1)} %reduce-scatter.3.cloned.1.call-done, bf16[4096,1024]{1,0:T(8,128)(2,1)} %param.8), kind=kOutput, calls=%fused_computation | convolution fusion | flops 6442450944 | bytes 22544384 | tf_op jit(solution)/shard_map/dot_general | solution.py:16
  248.4 0.0 reduce-scatter.5.cloned.1.call-update
  248.5 0.0 copy-start.2
  248.5 0.0 copy-start.4
  248.5 0.2 all-gather.10.cloned.1.call-start
  248.7 211.8 %reduce-scatter.5.cloned.1.call-done = f32[1024,768]{0,1:T(8,128)} async-done(((f32[4096,768]{0,1:T(8,128)}), f32[1024,768]{0,1:T(8,128)}) %reduce-scatter.5.cloned.1.call-update) | async-done | bytes 3145744 | tf_op jit(solution)/shard_map/reduce_scatter | solution.py:44
  460.5 3.3 convert_element_type.27
  463.8 0.0 all-gather.10.cloned.1.call-update
  463.8 0.0 copy-done.2
  463.8 0.2 copy.16
  464.0 0.0 copy-done.4
  464.0 0.2 reduce-window.7
  464.2 2.1 convert_bitcast_fusion.1
  466.3 1.6 copy.17
  467.9 43.5 %all-gather.10.cloned.1.call-done = bf16[4096,768]{0,1:T(8,128)(2,1)} async-done(((bf16[1024,768]{0,1:T(8,128)(2,1)}), bf16[4096,768]{0,1:T(8,128)(2,1)}) %all-gather.10.cloned.1.call-update) | async-done | bytes 6291472 | tf_op jit(solution)/shard_map/all_gather | solution.py:48
  511.4 0.0 copy-start.3
  511.4 3.6 copy.20
  514.9 0.0 copy-done.3
  514.9 0.0 copy-start.1
  515.0 1.9 fusion.13
  516.9 0.3 multiply_reduce_fusion
  517.1 0.2 fusion.8
  517.3 21.4 %psum.7 = f32[4,8]{1,0:T(4,128)S(1)} all-reduce(f32[4,8]{1,0:T(4,128)S(1)} %fusion.8), channel_id=1, replica_groups=mesh['grp'=4,'tile'=2,'arch'=4] {'grp','tile'}, use_global_device_ids=true, to_apply=%region_4.5 | all-reduce | flops 32 | bytes 256 | tf_op jit(solution)/shard_map/psum | solution.py:63
  538.7 0.6 broadcast_divide_fusion
  539.3 0.0 copy-done.1
  (2 shorter events, 0.0 us)
Async XLA Ops:
  7.2 175.8 %copy-start = (bf16[1536,768]{1,0:T(8,128)(2,1)S(1)}, bf16[1536,768]{1,0:T(8,128)(2,1)}, u32[]{:S(2)}) copy-start(bf16[1536,768]{1,0:T(8,128)(2,1)} %param.9) | copy-start | bytes 7077892
  7.2 120.5 %all-gather.8.cloned.1.call-start = ((), (), s32[]{:S(2)}) async-start(), calls=%async_computation.5 | async-start | bytes 7864320 | tf_op jit(solution)/shard_map/all_gather | solution.py:29
  7.9 175.1 %all-gather.6.cloned.1.call-start = ((), (), s32[]{:S(2)}) async-start(), calls=%async_computation.2 | async-start | bytes 4718592 | tf_op jit(solution)/shard_map/all_gather | solution.py:34
  139.7 96.5 %reduce-scatter.3.cloned.1.call-start = ((), (), s32[]{:S(2)}) async-start(), calls=%async_computation.3 | async-start | bytes 4718592 | tf_op jit(solution)/shard_map/reduce_scatter | solution.py:37
  192.6 267.9 %reduce-scatter.5.cloned.1.call-start = ((), (), s32[]{:S(2)}) async-start(), calls=%async_computation.4 | async-start | bytes 15728640 | tf_op jit(solution)/shard_map/reduce_scatter | solution.py:44
  248.5 215.3 %copy-start.2 = (bf16[256,768]{1,0:T(8,128)(2,1)S(1)}, bf16[256,768]{1,0:T(8,128)(2,1)}, u32[]{:S(2)}) copy-start(bf16[256,768]{1,0:T(8,128)(2,1)} %param.12) | copy-start | bytes 1179652
  248.5 215.5 %copy-start.4 = (s32[1,8]{1,0:T(1,128)S(1)}, s32[1,8]{1,0:T(1,128)}, u32[]{:S(2)}) copy-start(s32[1,8]{1,0:T(1,128)} %param.13) | copy-start | bytes 100
  248.5 262.9 %all-gather.10.cloned.1.call-start = ((), (), s32[]{:S(2)}) async-start(), calls=%async_computation.6 | async-start | bytes 7864320 | tf_op jit(solution)/shard_map/all_gather | solution.py:48
  511.4 3.6 copy-start.3
  514.9 24.3 %copy-start.1 = (bf16[1536,768]{1,0:T(8,128)(2,1)S(1)}, bf16[1536,768]{1,0:T(8,128)(2,1)}, u32[]{:S(2)}) copy-start(bf16[1536,768]{1,0:T(8,128)(2,1)} %param.9) | copy-start | bytes 7077892
Sparse Core Ops, SparseCore 0:
  9.6 118.0 all-gather.7
  139.8 43.0 all-gather.5
  192.8 43.4 reduce-scatter.2
  248.6 211.8 reduce-scatter.4
  463.9 47.3 all-gather.9
where the time goes:
time: 546 us
  waiting for transfers between devices  459 us (84%)
  matrix products  36 us (7%)
  blocking collectives  21.4 us (4%)
  between operations  13.9 us (3%)
  local copies, waits for them, and re-layouts  8.91 us (2%)
  other arithmetic  6.47 us (1%)
    reduce_scatter x1, waiting for transfers between devices, per_device(): lax.psum_scatter(contract_last(basis_part, restored), 'grp', scatter_dime...  212 us
    all_gather x1, waiting for transfers between devices, per_device(): lax.all_gather(local_query, 'grp', axis=1, tiled=True)  120 us
    reduce_scatter x1, waiting for transfers between devices, per_device(): lax.psum_scatter(jnp.dot(basis_part, scaled, preferred_element_type=jnp.f...  43.5 us
    all_gather x1, waiting for transfers between devices, per_device(): lax.all_gather(preconditioned[None], 'arch', axis=0, tiled=True)  43.5 us
    all_gather x1, waiting for transfers between devices, per_device(): lax.all_gather(rotated_in, 'tile', axis=0, tiled=True)  39.6 us
    psum x1, blocking collectives, per_device(): totals = lax.psum(partial_totals, ('grp', 'tile'))  21.4 us
    dot_general x1, matrix products, contract_last(): lax.dot_general(left_side, right_side, (((1,), (1,)), ((), ())), preferre...  12.2 us
    dot_general x1, matrix products, per_device(): jnp.dot(lax.all_gather(local_query, 'grp', axis=1, tiled=True), basis_par...  12 us
  transfers between devices with their start and end apart: 5, of which 5 were waited for; matrix products, arithmetic and copies ran while one was open for 1% of the time, Pallas kernels for 0%

commit v1 on v0

v1 whole, which is shorter than its diff:
```python
import jax
import jax.numpy as jnp
from jax import lax
from jax.sharding import PartitionSpec as P

damping = 0.01
f32 = jnp.float32
bf16 = jnp.bfloat16


def mm(a, b):
    return lax.dot_general(a, b, (((1,), (0,)), ((), ())), preferred_element_type=f32)


def mm_tn(a, b):
    return lax.dot_general(a, b, (((0,), (0,)), ((), ())), preferred_element_type=f32)


def mm_nt(a, b):
    return lax.dot_general(a, b, (((1,), (1,)), ((), ())), preferred_element_type=f32)


def folded(n):
    return [0] + list(range(1, n, 2)) + [i for i in range(n - 1, 0, -1) if i % 2 == 0]


def shift(x, axis, n, k):
    return lax.ppermute(x, axis, [(i, (i + k) % n) for i in range(n)])


def rows_at(x, start, size):
    return lax.dynamic_slice_in_dim(x, start, size, 0)


def cols_at(x, start, size):
    return lax.dynamic_slice_in_dim(x, start, size, 1)


def make(n_grp, n_tile, n_arch):
    ring = folded(n_grp)
    fw = [(ring[i], ring[(i + 1) % n_grp]) for i in range(n_grp)]
    bw = [(b, a) for a, b in fw]
    place = [ring.index(i) for i in range(n_grp)]

    def per_device(query_grads, input_basis, output_basis, eigenvalues, activations, gradients, seq_lengths):
        query = query_grads[0]
        nf, nd = query.shape
        width = nd // n_tile
        rows = activations.shape[0]
        grp, tile = lax.axis_index("grp"), lax.axis_index("tile")
        order = jnp.asarray(ring, jnp.int32)
        pos = jnp.asarray(place, jnp.int32)[grp]

        def at(k):
            return order[(pos + k) % n_grp]

        half = nf // 2
        top, low = query[:half], query[half:]
        own_rows = rows_at(input_basis, grp * nd, nd)
        acc_top, acc_low = mm(top, own_rows), mm(low, own_rows)
        for s in range(1, n_grp):
            top = lax.ppermute(top, "grp", fw)
            low = lax.ppermute(low, "grp", bw)
            acc_top += mm(top, rows_at(input_basis, at(-s) * nd, nd))
            acc_low += mm(low, rows_at(input_basis, at(s) * nd, nd))
        rotated_in = jnp.concatenate([acc_top.astype(bf16), acc_low.astype(bf16)], axis=0)

        bases, values = [output_basis], []
        for k in range(1, n_tile):
            bases.append(shift(output_basis, "tile", n_tile, k))
        values.append(cols_at(eigenvalues, tile * width, width))
        for k in range(1, n_tile):
            sent = cols_at(eigenvalues, ((tile + k) % n_tile) * width, width)
            values.append(shift(sent, "tile", n_tile, k))
        all_acts, all_grads = [activations], [gradients]
        for k in range(1, n_arch):
            all_acts.append(shift(activations, "arch", n_arch, k))
            all_grads.append(shift(gradients, "arch", n_arch, k))
        all_acts = jnp.concatenate(all_acts, axis=0)
        all_grads = jnp.concatenate(all_grads, axis=0)

        parts = [cols_at(rotated_in, tile * width, width)]
        for k in range(1, n_tile):
            sent = cols_at(rotated_in, ((tile + k) % n_tile) * width, width)
            parts.append(shift(sent, "tile", n_tile, k))
        scaled = []
        for basis, value in zip(bases, values):
            rotated = 0.0
            for k, part in enumerate(parts):
                rotated += mm_tn(rows_at(basis, ((tile - k) % n_tile) * nf, nf), part)
            scaled.append((rotated / (value + damping)).astype(bf16))
        back = []
        for k in range(n_tile):
            restored = 0.0
            for basis, one in zip(bases, scaled):
                restored += mm(rows_at(basis, ((tile + k) % n_tile) * nf, nf), one)
            restored = restored.astype(bf16)
            back.append(shift(restored, "tile", n_tile, k) if k else restored)
        restored = jnp.zeros((nf, nd), bf16)
        for k, one in enumerate(back):
            restored = lax.dynamic_update_slice_in_dim(restored, one, ((tile - k) % n_tile) * width, 1)

        hd = nd // 2

        def share(owner, low_half):
            return mm_nt(rows_at(input_basis, owner * nd + (hd if low_half else 0), hd), restored)

        top = share(at(-1), False).astype(bf16)
        low = share(at(1), True).astype(bf16)
        for s in range(2, n_grp + 1):
            top = lax.ppermute(top, "grp", fw)
            low = lax.ppermute(low, "grp", bw)
            top = (share(at(-s), False) + top.astype(f32)).astype(bf16)
            low = (share(at(s), True) + low.astype(f32)).astype(bf16)
        preconditioned = jnp.concatenate([top, low], axis=0)

        projected = mm(all_acts, preconditioned)
        tokens = jnp.sum(projected * all_grads.astype(f32), axis=1).reshape(n_arch, rows)
        token_parts = [tokens[0]]
        for k in range(1, n_arch):
            token_parts.append(shift(tokens[k], "arch", n_arch, n_arch - k))
        lengths = seq_lengths[0]
        ends = jnp.cumsum(lengths)
        starts = ends - lengths
        position = jnp.arange(rows, dtype=jnp.int32)
        member = ((position[None, :] >= starts[:, None]) & (position[None, :] < ends[:, None])).astype(f32)
        by_query = jnp.stack(token_parts, axis=0)
        by_query = jnp.roll(by_query, lax.axis_index("arch"), axis=0)
        totals = jnp.dot(by_query, member.T, precision=lax.Precision.HIGHEST)
        for axis, n in (("tile", n_tile), ("grp", n_grp)):
            totals = sum([shift(totals, axis, n, k) for k in range(1, n)], totals)
        return preconditioned[None], totals / lengths.astype(f32)[None, :]

    return per_device


def solution(mesh):
    n_grp, n_tile, n_arch = mesh.shape["grp"], mesh.shape["tile"], mesh.shape["arch"]
    return jax.shard_map(
        make(n_grp, n_tile, n_arch),
        mesh=mesh,
        in_specs=(
            P("arch", "tile", "grp"),
            P(None, "grp"),
            P(None, "tile"),
            P("tile", "grp"),
            P("arch", "grp"),
            P("arch", "tile"),
            P("arch", None),
        ),
        out_specs=(P("arch", "grp", "tile"), P(None, "arch")),
        check_vma=False,
    )
```

time: 546 us -> 337 us (0.62)
  waiting for transfers between devices: 459 us -> 217 us
  starting transfers between devices: 0.38 us -> 42.8 us
  blocking collectives: 21.4 us -> 0 us
  matrix products: 36 us -> 56.9 us
    reduce_scatter x2 -> x0, waiting for transfers between devices: 255 us -> none  [the longest x1 212 us: per_device(): lax.psum_scatter(contract_last(basis_part, restored), 'grp', scatter_dime...]
    ppermute x0 -> x29, waiting for transfers between devices: none -> 217 us  [the longest x6 91 us: per_device(): top = lax.ppermute(top, 'grp', fw)]
    all_gather x3 -> x0, waiting for transfers between devices: 203 us -> none  [the longest x1 120 us: per_device(): lax.all_gather(local_query, 'grp', axis=1, tiled=True)]
    ppermute x0 -> x29, starting transfers between devices: none -> 42.8 us  [the longest x17 18.4 us: shift(): return lax.ppermute(x, axis, [(i, (i + k) % n) for i in range(n)])]
    psum x1 -> x0, blocking collectives: 21.4 us -> none  [per_device(): totals = lax.psum(partial_totals, ('grp', 'tile'))]
    dot_general x5 -> x26, matrix products: 36 us -> 56.9 us  [the longest x13 25.1 us: mm(): lax.dot_general(a, b, (((1,), (0,)), ((), ())), preferred_element_type=f32)]
  transfers between devices with their start and end apart: 5 -> 29, of which waited for: 5 -> 24; matrix products, arithmetic and copies ran while one was open for 1% -> 15% of each run, Pallas kernels for 0% -> 0%
where the time goes in v1:
time: 337 us; the launch traced here: 336 us
  waiting for transfers between devices  217 us (64%)
  matrix products  56.9 us (17%)
  starting transfers between devices  42.8 us (13%)
  between operations  11.4 us (3%)
  local copies, waits for them, and re-layouts  5.47 us (2%)
    ppermute x6, waiting for transfers between devices, per_device(): top = lax.ppermute(top, 'grp', fw)  91 us
    ppermute x17, waiting for transfers between devices, shift(): return lax.ppermute(x, axis, [(i, (i + k) % n) for i in range(n)])  82.9 us
    ppermute x6, waiting for transfers between devices, per_device(): low = lax.ppermute(low, 'grp', bw)  42.7 us
    dot_general x13, matrix products, mm(): lax.dot_general(a, b, (((1,), (0,)), ((), ())), preferred_element_type=f32)  25.1 us
    dot_general x8, matrix products, mm_nt(): lax.dot_general(a, b, (((1,), (1,)), ((), ())), preferred_element_type=f32)  22.3 us
    ppermute x17, starting transfers between devices, shift(): return lax.ppermute(x, axis, [(i, (i + k) % n) for i in range(n)])  18.4 us
    ppermute x6, starting transfers between devices, per_device(): low = lax.ppermute(low, 'grp', bw)  13 us
    ppermute x6, starting transfers between devices, per_device(): top = lax.ppermute(top, 'grp', fw)  11.4 us
  transfers between devices with their start and end apart: 29, of which 24 were waited for; matrix products, arithmetic and copies ran while one was open for 15% of the time, Pallas kernels for 0%

profile of v1, /device:TPU:0, one launch (start us, length us, event | category | flops | bytes accessed | tf_op | source)
XLA Modules:
  0.0 336.2 jit_solution(5482029094305996984)
XLA Ops:
  0.7 1.6 slice_bitcast_fusion
  2.3 4.1 %collective-permute-start.3 = (bf16[384,1024]{1,0:T(8,128)(2,1)S(1)}, bf16[384,1024]{1,0:T(8,128)(2,1)}, u32[]{:S(2)}, u32[]{:S(2)}) collective-permute-start(bf16[384,1024]{1,0:T(8,128)(2,1)S(1)} %get-tuple-element.2), channel_id=1, source_target_pairs={{8,0},{24,8},{16,24},{0,16},{9,1},{25,9},{17,25},{1,17},{10,2},{26... | collective-permute-start | bytes 2359304 | tf_op jit(solution)/shard_map/ppermute | solution.py:63
  6.4 1.5 collective-permute-start.7
  18.4 6.0 %collective-permute-done.3 = bf16[384,1024]{1,0:T(8,128)(2,1)} collective-permute-done((bf16[384,1024]{1,0:T(8,128)(2,1)S(1)}, bf16[384,1024]{1,0:T(8,128)(2,1)}, u32[]{:S(2)}, u32[]{:S(2)}) %collective-permute-start.3) | collective-permute-done | bytes 786464 | tf_op jit(solution)/shard_map/ppermute | solution.py:63
  24.4 3.5 %collective-permute-start.4 = (bf16[384,1024]{1,0:T(8,128)(2,1)}, bf16[384,1024]{1,0:T(8,128)(2,1)S(1)}, u32[]{:S(2)}, u32[]{:S(2)}) collective-permute-start(bf16[384,1024]{1,0:T(8,128)(2,1)} %collective-permute-done.3), channel_id=1, source_target_pairs={{8,0},{24,8},{16,24},{0,16},{9,1},{25,9},{17,25},{1,17},{10,2},{26... | collective-permute-start | bytes 2359304 | tf_op jit(solution)/shard_map/ppermute | solution.py:63
  27.8 2.7 fusion.22
  30.6 12.6 %collective-permute-done = bf16[384,1024]{1,0:T(8,128)(2,1)} collective-permute-done((bf16[384,1024]{1,0:T(8,128)(2,1)S(1)}, bf16[384,1024]{1,0:T(8,128)(2,1)}, u32[]{:S(2)}, u32[]{:S(2)}) %collective-permute-start) | collective-permute-done | bytes 786464 | tf_op jit(solution)/shard_map/ppermute | solution.py:62
  43.8 2.6 fusion.20
  46.4 2.1 fusion.12
  48.5 10.9 %collective-permute-done.4 = bf16[384,1024]{1,0:T(8,128)(2,1)S(1)} collective-permute-done((bf16[384,1024]{1,0:T(8,128)(2,1)}, bf16[384,1024]{1,0:T(8,128)(2,1)S(1)}, u32[]{:S(2)}, u32[]{:S(2)}) %collective-permute-start.4) | collective-permute-done | bytes 786464 | tf_op jit(solution)/shard_map/ppermute | solution.py:63
  59.4 2.1 collective-permute-start.5
  61.5 2.1 fusion.18
  63.6 13.1 %collective-permute-done.1 = bf16[384,1024]{1,0:T(8,128)(2,1)S(1)} collective-permute-done((bf16[384,1024]{1,0:T(8,128)(2,1)}, bf16[384,1024]{1,0:T(8,128)(2,1)S(1)}, u32[]{:S(2)}, u32[]{:S(2)}) %collective-permute-start.1) | collective-permute-done | bytes 786464 | tf_op jit(solution)/shard_map/ppermute | solution.py:62
  77.4 1.0 fusion.10
  78.4 1.0 fusion.16
  79.4 14.1 %collective-permute-done.5 = bf16[384,1024]{1,0:T(8,128)(2,1)S(1)} collective-permute-done((bf16[384,1024]{1,0:T(8,128)(2,1)S(1)}, bf16[384,1024]{1,0:T(8,128)(2,1)S(1)}, u32[]{:S(2)}, u32[]{:S(2)}) %collective-permute-start.5) | collective-permute-done | bytes 786464 | tf_op jit(solution)/shard_map/ppermute | solution.py:63
  93.6 1.0 fusion.32
  94.6 14.7 %collective-permute-done.2 = bf16[384,1024]{1,0:T(8,128)(2,1)S(1)} collective-permute-done((bf16[384,1024]{1,0:T(8,128)(2,1)S(1)}, bf16[384,1024]{1,0:T(8,128)(2,1)S(1)}, u32[]{:S(2)}, u32[]{:S(2)}) %collective-permute-start.2) | collective-permute-done | bytes 786464 | tf_op jit(solution)/shard_map/ppermute | solution.py:62
  109.3 1.0 fusion.29
  110.4 1.0 fusion.58
  111.3 1.5 collective-permute-start.6
  113.6 2.2 fusion.53
  115.8 16.3 %collective-permute-done.6 = bf16[768,512]{1,0:T(8,128)(2,1)} collective-permute-done((bf16[768,512]{1,0:T(8,128)(2,1)}, bf16[768,512]{1,0:T(8,128)(2,1)}, u32[]{:S(2)}, u32[]{:S(2)}) %collective-permute-start.6) | collective-permute-done | bytes 786464 | tf_op jit(solution)/shard_map/ppermute | solution.py:28
  132.1 2.3 divide_convert_fusion.1
  135.3 2.3 fusion.38
  137.6 27.2 %collective-permute-done.8 = f32[768,512]{1,0:T(8,128)} collective-permute-done((f32[768,512]{1,0:T(8,128)S(1)}, f32[768,512]{1,0:T(8,128)}, u32[]{:S(2)}, u32[]{:S(2)}) %collective-permute-start.8) | collective-permute-done | bytes 1572896 | tf_op jit(solution)/shard_map/ppermute | solution.py:28
  164.8 2.6 divide_convert_fusion
  168.3 2.1 add_convert_fusion.6
  170.4 1.6 collective-permute-start.9
  172.1 2.0 fusion.51
  174.3 0.9 copy-done.12
  175.2 2.0 fusion.28
  177.3 11.9 %collective-permute-done.9 = bf16[768,512]{1,0:T(8,128)(2,1)S(1)} collective-permute-done((bf16[768,512]{1,0:T(8,128)(2,1)S(1)}, bf16[768,512]{1,0:T(8,128)(2,1)S(1)}, u32[]{:S(2)}, u32[]{:S(2)}) %collective-permute-start.9) | collective-permute-done | bytes 786464 | tf_op jit(solution)/shard_map/ppermute | solution.py:28
  189.2 2.3 convolution_convert_fusion.1
  191.6 3.1 convolution_convert_fusion
  194.7 2.9 collective-permute-start.13
  197.6 27.5 %collective-permute-done.10 = bf16[512,768]{1,0:T(8,128)(2,1)S(1)} collective-permute-done((bf16[512,768]{1,0:T(8,128)(2,1)S(1)}, bf16[512,768]{1,0:T(8,128)(2,1)S(1)}, u32[]{:S(2)}, u32[]{:S(2)}) %collective-permute-start.10) | collective-permute-done | bytes 786464 | tf_op jit(solution)/shard_map/ppermute | solution.py:111
  225.1 2.2 add_convert_fusion.5
  227.4 2.5 collective-permute-start.11
  229.9 3.4 add_convert_fusion.2
  233.7 22.1 %collective-permute-done.11 = bf16[512,768]{1,0:T(8,128)(2,1)S(1)} collective-permute-done((bf16[512,768]{1,0:T(8,128)(2,1)S(1)}, bf16[512,768]{1,0:T(8,128)(2,1)S(1)}, u32[]{:S(2)}, u32[]{:S(2)}) %collective-permute-start.11) | collective-permute-done | bytes 786464 | tf_op jit(solution)/shard_map/ppermute | solution.py:111
  255.8 3.1 add_convert_fusion.4
  259.0 7.4 %collective-permute-start.12 = (bf16[512,768]{1,0:T(8,128)(2,1)}, bf16[512,768]{1,0:T(8,128)(2,1)S(1)}, u32[]{:S(2)}, u32[]{:S(2)}) collective-permute-start(bf16[512,768]{1,0:T(8,128)(2,1)} %add_convert_fusion.4), channel_id=1, source_target_pairs={{0,8},{8,24},{24,16},{16,0},{1,9},{9,25},{25,17},{17,1},{2,10},{10... | collective-permute-start | bytes 2359304 | tf_op jit(solution)/shard_map/ppermute | solution.py:111
  266.4 2.1 collective-permute-done.14
  268.5 3.4 add_convert_fusion.1
  272.1 1.6 collective-permute-start.20
  273.6 1.4 collective-permute-start.21
  276.5 6.4 %collective-permute-done.19 = bf16[256,768]{0,1:T(8,128)(2,1)S(1)} collective-permute-done((bf16[256,768]{0,1:T(8,128)(2,1)S(1)}, bf16[256,768]{0,1:T(8,128)(2,1)S(1)}, u32[]{:S(2)}, u32[]{:S(2)}) %collective-permute-start.19) | collective-permute-done | bytes 393248 | tf_op jit(solution)/shard_map/ppermute | solution.py:28
  283.7 1.5 collective-permute-start.17
  285.2 9.6 %collective-permute-done.15 = bf16[512,768]{1,0:T(8,128)(2,1)} collective-permute-done((bf16[512,768]{1,0:T(8,128)(2,1)}, bf16[512,768]{1,0:T(8,128)(2,1)}, u32[]{:S(2)}, u32[]{:S(2)}) %collective-permute-start.15) | collective-permute-done | bytes 786464 | tf_op jit(solution)/shard_map/ppermute | solution.py:112
  294.9 2.2 add_convert_fusion.3
  297.1 2.6 add_convert_fusion
  299.7 2.8 collective-permute-done.16
  302.5 1.3 collective-permute-done.17
  303.8 9.7 %collective-permute-done.18 = bf16[256,1024]{1,0:T(8,128)(2,1)S(1)} collective-permute-done((bf16[256,1024]{1,0:T(8,128)(2,1)}, bf16[256,1024]{1,0:T(8,128)(2,1)S(1)}, u32[]{:S(2)}, u32[]{:S(2)}) %collective-permute-start.18) | collective-permute-done | bytes 524320 | tf_op jit(solution)/shard_map/ppermute | solution.py:28
  313.5 4.5 %multiply_reduce_fusion = f32[1024]{0:T(1024)S(1)} fusion(bf16[256,768]{0,1:T(8,128)(2,1)} %collective-permute-done.21, bf16[256,768]{0,1:T(8,128)(2,1)} %collective-permute-done.20, bf16[256,768]{0,1:T(8,128)(2,1)S(1)} %copy-done.9, bf16[256,768]{0,1:T(8,128)(2,1)S(1)} %copy.14, bf16[256,1024]{1,0:T(8,128)(2,1)S(1)} %collective-permute-done.18, ...), kind=kOutput, calls=%fused_computation | convolution fusion | flops 1630010368 | bytes 5246976 | tf_op jit(solution)/shard_map/dot_general | solution.py:12
  318.1 1.9 collective-permute-start.22
  321.2 2.3 collective-permute-done.23
  323.7 1.5 collective-permute-start.25
  325.2 1.2 fusion.57
  327.3 2.0 collective-permute-start.26
  329.3 2.7 collective-permute-start.27
  332.1 0.9 collective-permute-done.26
  333.8 1.8 collective-permute-done.28
  (66 shorter events, 11.1 us)
Async XLA Ops:
  0.6 7.3 %copy-start.5 = (s32[4]{0:T(128)S(1)}, s32[4]{0:T(128)}, u32[]{:S(2)}) copy-start(s32[4]{0:T(128)} %constant.181.clone) | copy-start | bytes 52
  0.6 27.2 %copy-start.1 = (bf16[1,768,1024]{2,1,0:T(8,128)(2,1)S(1)}, bf16[1,768,1024]{2,1,0:T(8,128)(2,1)}, u32[]{:S(2)}) copy-start(bf16[1,768,1024]{2,1,0:T(8,128)(2,1)} %param.9) | copy-start | bytes 4718596
  2.3 22.1 %collective-permute-start.3 = (bf16[384,1024]{1,0:T(8,128)(2,1)S(1)}, bf16[384,1024]{1,0:T(8,128)(2,1)}, u32[]{:S(2)}, u32[]{:S(2)}) collective-permute-start(bf16[384,1024]{1,0:T(8,128)(2,1)S(1)} %get-tuple-element.2), channel_id=1, source_target_pairs={{8,0},{24,8},{16,24},{0,16},{9,1},{25,9},{17,25},{1,17},{10,2},{26... | collective-permute-start | bytes 2359304 | tf_op jit(solution)/shard_map/ppermute | solution.py:63
  6.4 36.7 %collective-permute-start = (bf16[384,1024]{1,0:T(8,128)(2,1)S(1)}, bf16[384,1024]{1,0:T(8,128)(2,1)}, u32[]{:S(2)}, u32[]{:S(2)}) collective-permute-start(bf16[384,1024]{1,0:T(8,128)(2,1)S(1)} %get-tuple-element.3), channel_id=1, source_target_pairs={{0,8},{8,24},{24,16},{16,0},{1,9},{9,25},{25,17},{17,1},{2,10},{10... | collective-permute-start | bytes 2359304 | tf_op jit(solution)/shard_map/ppermute | solution.py:62
  6.4 128.9 %collective-permute-start.7 = (bf16[1536,768]{1,0:T(8,128)(2,1)}, bf16[1536,768]{1,0:T(8,128)(2,1)}, u32[]{:S(2)}, u32[]{:S(2)}) collective-permute-start(bf16[1536,768]{1,0:T(8,128)(2,1)} %param.11), channel_id=1, source_target_pairs={{0,4},{4,0},{1,5},{5,1},{2,6},{6,2},{3,7},{7,3},{8,12},{12,8},{9,1... | collective-permute-start | bytes 7077896 | tf_op jit(solution)/shard_map/ppermute | solution.py:28
  24.4 35.0 %collective-permute-start.4 = (bf16[384,1024]{1,0:T(8,128)(2,1)}, bf16[384,1024]{1,0:T(8,128)(2,1)S(1)}, u32[]{:S(2)}, u32[]{:S(2)}) collective-permute-start(bf16[384,1024]{1,0:T(8,128)(2,1)} %collective-permute-done.3), channel_id=1, source_target_pairs={{8,0},{24,8},{16,24},{0,16},{9,1},{25,9},{17,25},{1,17},{10,2},{26... | collective-permute-start | bytes 2359304 | tf_op jit(solution)/shard_map/ppermute | solution.py:63
  27.8 18.5 %copy-start = (bf16[4096,1024]{1,0:T(8,128)(2,1)S(1)}, bf16[4096,1024]{1,0:T(8,128)(2,1)}, u32[]{:S(2)}) copy-start(bf16[4096,1024]{1,0:T(8,128)(2,1)} %param.10) | copy-start | bytes 25165828
  43.1 33.6 %collective-permute-start.1 = (bf16[384,1024]{1,0:T(8,128)(2,1)}, bf16[384,1024]{1,0:T(8,128)(2,1)S(1)}, u32[]{:S(2)}, u32[]{:S(2)}) collective-permute-start(bf16[384,1024]{1,0:T(8,128)(2,1)} %collective-permute-done), channel_id=1, source_target_pairs={{0,8},{8,24},{24,16},{16,0},{1,9},{9,25},{25,17},{17,1},{2,10},{10... | collective-permute-start | bytes 2359304 | tf_op jit(solution)/shard_map/ppermute | solution.py:62
  59.4 34.2 %collective-permute-start.5 = (bf16[384,1024]{1,0:T(8,128)(2,1)S(1)}, bf16[384,1024]{1,0:T(8,128)(2,1)S(1)}, u32[]{:S(2)}, u32[]{:S(2)}) collective-permute-start(bf16[384,1024]{1,0:T(8,128)(2,1)S(1)} %collective-permute-done.4), channel_id=1, source_target_pairs={{8,0},{24,8},{16,24},{0,16},{9,1},{25,9},{17,25},{1,17},{10,2},{26... | collective-permute-start | bytes 2359304 | tf_op jit(solution)/shard_map/ppermute | solution.py:63
  76.8 32.6 %collective-permute-start.2 = (bf16[384,1024]{1,0:T(8,128)(2,1)S(1)}, bf16[384,1024]{1,0:T(8,128)(2,1)S(1)}, u32[]{:S(2)}, u32[]{:S(2)}) collective-permute-start(bf16[384,1024]{1,0:T(8,128)(2,1)S(1)} %collective-permute-done.1), channel_id=1, source_target_pairs={{0,8},{8,24},{24,16},{16,0},{1,9},{9,25},{25,17},{17,1},{2,10},{10... | collective-permute-start | bytes 2359304 | tf_op jit(solution)/shard_map/ppermute | solution.py:62
  109.3 3.5 %copy-start.2 = (f32[768,1024]{1,0:T(8,128)S(1)}, f32[768,1024]{1,0:T(8,128)}, u32[]{:S(2)}) copy-start(f32[768,1024]{1,0:T(8,128)} %param.12) | copy-start | bytes 9437188
  111.3 20.7 %collective-permute-start.6 = (bf16[768,512]{1,0:T(8,128)(2,1)}, bf16[768,512]{1,0:T(8,128)(2,1)}, u32[]{:S(2)}, u32[]{:S(2)}) collective-permute-start(bf16[768,512]{1,0:T(8,128)(2,1)} %fusion.58), channel_id=1, source_target_pairs={{0,4},{4,0},{1,5},{5,1},{2,6},{6,2},{3,7},{7,3},{8,12},{12,8},{9,1... | collective-permute-start | bytes 2359304 | tf_op jit(solution)/shard_map/ppermute | solution.py:28
  113.0 51.8 %collective-permute-start.8 = (f32[768,512]{1,0:T(8,128)S(1)}, f32[768,512]{1,0:T(8,128)}, u32[]{:S(2)}, u32[]{:S(2)}) collective-permute-start(f32[768,512]{1,0:T(8,128)S(1)} %constant_dynamic-slice_fusion.1), channel_id=1, source_target_pairs={{0,4},{4,0},{1,5},{5,1},{2,6},{6,2},{3,7},{7,3},{8,12},{12,8},{9,1... | collective-permute-start | bytes 4718600 | tf_op jit(solution)/shard_map/ppermute | solution.py:28
  113.5 18.5 %copy-start.3 = (f32[768,1024]{1,0:T(8,128)S(1)}, f32[768,1024]{1,0:T(8,128)}, u32[]{:S(2)}) copy-start(f32[768,1024]{1,0:T(8,128)} %param.12) | copy-start | bytes 9437188
  115.8 18.6 %copy-start.6 = (bf16[1536,768]{1,0:T(8,128)(2,1)S(1)}, bf16[1536,768]{1,0:T(8,128)(2,1)}, u32[]{:S(2)}) copy-start(bf16[1536,768]{1,0:T(8,128)(2,1)} %param.11) | copy-start | bytes 7077892
  134.4 0.9 copy-start.13
  167.4 0.9 copy-start.11
  168.3 3.7 %copy-start.14 = (bf16[768,512]{1,0:T(8,128)(2,1)S(1)}, bf16[768,512]{1,0:T(8,128)(2,1)}, u32[]{:S(2)}) copy-start(bf16[768,512]{1,0:T(8,128)(2,1)} %copy-done.13) | copy-start | bytes 2359300
  170.4 18.7 %collective-permute-start.9 = (bf16[768,512]{1,0:T(8,128)(2,1)S(1)}, bf16[768,512]{1,0:T(8,128)(2,1)S(1)}, u32[]{:S(2)}, u32[]{:S(2)}) collective-permute-start(bf16[768,512]{1,0:T(8,128)(2,1)S(1)} %add_convert_fusion.6), channel_id=1, source_target_pairs={{0,4},{4,0},{1,5},{5,1},{2,6},{6,2},{3,7},{7,3},{8,12},{12,8},{9,1... | collective-permute-start | bytes 2359304 | tf_op jit(solution)/shard_map/ppermute | solution.py:28
  174.1 1.1 copy-start.12
  191.5 33.6 %collective-permute-start.10 = (bf16[512,768]{1,0:T(8,128)(2,1)S(1)}, bf16[512,768]{1,0:T(8,128)(2,1)S(1)}, u32[]{:S(2)}, u32[]{:S(2)}) collective-permute-start(bf16[512,768]{1,0:T(8,128)(2,1)S(1)} %convolution_convert_fusion.1), channel_id=1, source_target_pairs={{0,8},{8,24},{24,16},{16,0},{1,9},{9,25},{25,17},{17,1},{2,10},{10... | collective-permute-start | bytes 2359304 | tf_op jit(solution)/shard_map/ppermute | solution.py:111
  194.7 35.2 %collective-permute-start.13 = (bf16[512,768]{1,0:T(8,128)(2,1)}, bf16[512,768]{1,0:T(8,128)(2,1)}, u32[]{:S(2)}, u32[]{:S(2)}) collective-permute-start(bf16[512,768]{1,0:T(8,128)(2,1)} %convolution_convert_fusion), channel_id=1, source_target_pairs={{8,0},{24,8},{16,24},{0,16},{9,1},{25,9},{17,25},{1,17},{10,2},{26... | collective-permute-start | bytes 2359304 | tf_op jit(solution)/shard_map/ppermute | solution.py:112
  227.4 28.5 %collective-permute-start.11 = (bf16[512,768]{1,0:T(8,128)(2,1)S(1)}, bf16[512,768]{1,0:T(8,128)(2,1)S(1)}, u32[]{:S(2)}, u32[]{:S(2)}) collective-permute-start(bf16[512,768]{1,0:T(8,128)(2,1)S(1)} %add_convert_fusion.5), channel_id=1, source_target_pairs={{0,8},{8,24},{24,16},{16,0},{1,9},{9,25},{25,17},{17,1},{2,10},{10... | collective-permute-start | bytes 2359304 | tf_op jit(solution)/shard_map/ppermute | solution.py:111
  233.2 35.2 %collective-permute-start.14 = (bf16[512,768]{1,0:T(8,128)(2,1)}, bf16[512,768]{1,0:T(8,128)(2,1)}, u32[]{:S(2)}, u32[]{:S(2)}) collective-permute-start(bf16[512,768]{1,0:T(8,128)(2,1)} %add_convert_fusion.2), channel_id=1, source_target_pairs={{8,0},{24,8},{16,24},{0,16},{9,1},{25,9},{17,25},{1,17},{10,2},{26... | collective-permute-start | bytes 2359304 | tf_op jit(solution)/shard_map/ppermute | solution.py:112
  258.9 12.9 %copy-start.4 = (bf16[256,768]{1,0:T(8,128)(2,1)S(1)}, bf16[256,768]{1,0:T(8,128)(2,1)}, u32[]{:S(2)}) copy-start(bf16[256,768]{1,0:T(8,128)(2,1)} %param.14) | copy-start | bytes 1179652
  259.0 17.3 %copy-start.10 = (s32[1,8]{1,0:T(1,128)S(1)}, s32[1,8]{1,0:T(1,128)}, u32[]{:S(2)}) copy-start(s32[1,8]{1,0:T(1,128)} %param.15) | copy-start | bytes 100
  259.0 24.8 %collective-permute-start.12 = (bf16[512,768]{1,0:T(8,128)(2,1)}, bf16[512,768]{1,0:T(8,128)(2,1)S(1)}, u32[]{:S(2)}, u32[]{:S(2)}) collective-permute-start(bf16[512,768]{1,0:T(8,128)(2,1)} %add_convert_fusion.4), channel_id=1, source_target_pairs={{0,8},{8,24},{24,16},{16,0},{1,9},{9,25},{25,17},{17,1},{2,10},{10... | collective-permute-start | bytes 2359304 | tf_op jit(solution)/shard_map/ppermute | solution.py:111
  271.8 23.0 %collective-permute-start.15 = (bf16[512,768]{1,0:T(8,128)(2,1)}, bf16[512,768]{1,0:T(8,128)(2,1)}, u32[]{:S(2)}, u32[]{:S(2)}) collective-permute-start(bf16[512,768]{1,0:T(8,128)(2,1)} %add_convert_fusion.1), channel_id=1, source_target_pairs={{8,0},{24,8},{16,24},{0,16},{9,1},{25,9},{17,25},{1,17},{10,2},{26... | collective-permute-start | bytes 2359304 | tf_op jit(solution)/shard_map/ppermute | solution.py:112
  272.0 10.8 %collective-permute-start.19 = (bf16[256,768]{0,1:T(8,128)(2,1)S(1)}, bf16[256,768]{0,1:T(8,128)(2,1)S(1)}, u32[]{:S(2)}, u32[]{:S(2)}) collective-permute-start(bf16[256,768]{0,1:T(8,128)(2,1)S(1)} %copy.14), channel_id=1, source_target_pairs={{0,1},{1,2},{2,3},{3,0},{4,5},{5,6},{6,7},{7,4},{8,9},{9,10},{10,1... | collective-permute-start | bytes 1179656 | tf_op jit(solution)/shard_map/ppermute | solution.py:28
  272.1 27.6 %collective-permute-start.20 = (bf16[256,768]{0,1:T(8,128)(2,1)S(1)}, bf16[256,768]{0,1:T(8,128)(2,1)}, u32[]{:S(2)}, u32[]{:S(2)}) collective-permute-start(bf16[256,768]{0,1:T(8,128)(2,1)S(1)} %copy.14), channel_id=1, source_target_pairs={{0,2},{1,3},{2,0},{3,1},{4,6},{5,7},{6,4},{7,5},{8,10},{9,11},{10,... | collective-permute-start | bytes 1179656 | tf_op jit(solution)/shard_map/ppermute | solution.py:28
  273.6 26.1 %collective-permute-start.21 = (bf16[256,768]{0,1:T(8,128)(2,1)S(1)}, bf16[256,768]{0,1:T(8,128)(2,1)}, u32[]{:S(2)}, u32[]{:S(2)}) collective-permute-start(bf16[256,768]{0,1:T(8,128)(2,1)S(1)} %copy.14), channel_id=1, source_target_pairs={{0,3},{1,0},{2,1},{3,2},{4,7},{5,4},{6,5},{7,6},{8,11},{9,8},{10,9... | collective-permute-start | bytes 1179656 | tf_op jit(solution)/shard_map/ppermute | solution.py:28
  282.8 12.0 %copy-start.8 = (bf16[256,768]{0,1:T(8,128)(2,1)}, bf16[256,768]{0,1:T(8,128)(2,1)S(1)}, u32[]{:S(2)}) copy-start(bf16[256,768]{0,1:T(8,128)(2,1)S(1)} %collective-permute-done.19) | copy-start | bytes 1179652
  282.8 19.7 %collective-permute-start.16 = (bf16[256,1024]{1,0:T(8,128)(2,1)}, bf16[256,1024]{1,0:T(8,128)(2,1)S(1)}, u32[]{:S(2)}, u32[]{:S(2)}) collective-permute-start(bf16[256,1024]{1,0:T(8,128)(2,1)} %param.13), channel_id=1, source_target_pairs={{0,1},{1,2},{2,3},{3,0},{4,5},{5,6},{6,7},{7,4},{8,9},{9,10},{10,1... | collective-permute-start | bytes 1572872 | tf_op jit(solution)/shard_map/ppermute | solution.py:28
  283.7 20.1 %collective-permute-start.17 = (bf16[256,1024]{1,0:T(8,128)(2,1)}, bf16[256,1024]{1,0:T(8,128)(2,1)S(1)}, u32[]{:S(2)}, u32[]{:S(2)}) collective-permute-start(bf16[256,1024]{1,0:T(8,128)(2,1)} %param.13), channel_id=1, source_target_pairs={{0,2},{1,3},{2,0},{3,1},{4,6},{5,7},{6,4},{7,5},{8,10},{9,11},{10,... | collective-permute-start | bytes 1572872 | tf_op jit(solution)/shard_map/ppermute | solution.py:28
  294.9 18.6 %collective-permute-start.18 = (bf16[256,1024]{1,0:T(8,128)(2,1)}, bf16[256,1024]{1,0:T(8,128)(2,1)S(1)}, u32[]{:S(2)}, u32[]{:S(2)}) collective-permute-start(bf16[256,1024]{1,0:T(8,128)(2,1)} %param.13), channel_id=1, source_target_pairs={{0,3},{1,0},{2,1},{3,2},{4,7},{5,4},{6,5},{7,6},{8,11},{9,8},{10,9... | collective-permute-start | bytes 1572872 | tf_op jit(solution)/shard_map/ppermute | solution.py:28
  297.1 16.4 %copy-start.7 = (bf16[256,1024]{1,0:T(8,128)(2,1)S(1)}, bf16[256,1024]{1,0:T(8,128)(2,1)}, u32[]{:S(2)}) copy-start(bf16[256,1024]{1,0:T(8,128)(2,1)} %param.13) | copy-start | bytes 1572868
  297.1 16.4 %copy-start.9 = (bf16[256,768]{0,1:T(8,128)(2,1)S(1)}, bf16[256,768]{0,1:T(8,128)(2,1)}, u32[]{:S(2)}) copy-start(bf16[256,768]{0,1:T(8,128)(2,1)} %copy-done.8) | copy-start | bytes 1179652
  318.1 3.2 collective-permute-start.22
  319.9 3.6 %collective-permute-start.23 = (f32[256]{0:T(256)S(1)}, f32[256]{0:T(256)S(1)}, u32[]{:S(2)}, u32[]{:S(2)}) collective-permute-start(f32[256]{0:T(256)S(1)} %get-tuple-element.5), channel_id=1, source_target_pairs={{0,2},{1,3},{2,0},{3,1},{4,6},{5,7},{6,4},{7,5},{8,10},{9,11},{10,... | collective-permute-start | bytes 3080 | tf_op jit(solution)/shard_map/ppermute | solution.py:28
  320.5 3.0 collective-permute-start.24
  323.7 3.6 %collective-permute-start.25 = (f32[4,8]{1,0:T(4,128)S(1)}, f32[4,8]{1,0:T(4,128)S(1)}, u32[]{:S(2)}, u32[]{:S(2)}) collective-permute-start(f32[4,8]{1,0:T(4,128)S(1)} %fusion.61), channel_id=1, source_target_pairs={{0,4},{4,0},{1,5},{5,1},{2,6},{6,2},{3,7},{7,3},{8,12},{12,8},{9,1... | collective-permute-start | bytes 392 | tf_op jit(solution)/shard_map/ppermute | solution.py:28
  327.3 5.7 %collective-permute-start.26 = (f32[4,8]{1,0:T(4,128)S(1)}, f32[4,8]{1,0:T(4,128)S(1)}, u32[]{:S(2)}, u32[]{:S(2)}) collective-permute-start(f32[4,8]{1,0:T(4,128)S(1)} %add.400), channel_id=1, source_target_pairs={{0,8},{8,16},{16,24},{24,0},{1,9},{9,17},{17,25},{25,1},{2,10},{10... | collective-permute-start | bytes 392 | tf_op jit(solution)/shard_map/ppermute | solution.py:28
  329.3 4.5 %collective-permute-start.27 = (f32[4,8]{1,0:T(4,128)S(1)}, f32[4,8]{1,0:T(4,128)S(1)}, u32[]{:S(2)}, u32[]{:S(2)}) collective-permute-start(f32[4,8]{1,0:T(4,128)S(1)} %add.400), channel_id=1, source_target_pairs={{0,16},{8,24},{16,0},{24,8},{1,17},{9,25},{17,1},{25,9},{2,18},{10... | collective-permute-start | bytes 392 | tf_op jit(solution)/shard_map/ppermute | solution.py:28
  332.0 3.6 %collective-permute-start.28 = (f32[4,8]{1,0:T(4,128)S(1)}, f32[4,8]{1,0:T(4,128)S(1)}, u32[]{:S(2)}, u32[]{:S(2)}) collective-permute-start(f32[4,8]{1,0:T(4,128)S(1)} %add.400), channel_id=1, source_target_pairs={{0,24},{8,0},{16,8},{24,16},{1,25},{9,1},{17,9},{25,17},{2,26},{10... | collective-permute-start | bytes 392 | tf_op jit(solution)/shard_map/ppermute | solution.py:28

commit v2 on v1

v2 whole, which is shorter than its diff:
```python
import jax
import jax.numpy as jnp
from jax import lax
from jax.experimental import pallas as pl
from jax.experimental.pallas import tpu as pltpu
from jax.sharding import PartitionSpec as P

damping = 0.01
f32 = jnp.float32
bf16 = jnp.bfloat16


def mm(a, b):
    return lax.dot_general(a, b, (((1,), (0,)), ((), ())), preferred_element_type=f32)


def mm_tn(a, b):
    return lax.dot_general(a, b, (((0,), (0,)), ((), ())), preferred_element_type=f32)


def mm_tt(a, b):
    return lax.dot_general(a, b, (((0,), (1,)), ((), ())), preferred_element_type=f32)


def folded(n):
    return [0] + list(range(1, n, 2)) + [i for i in range(n - 1, 0, -1) if i % 2 == 0]


def rows_at(x, start, size):
    return lax.dynamic_slice_in_dim(x, start, size, 0)


def cols_at(x, start, size):
    return lax.dynamic_slice_in_dim(x, start, size, 1)


def assemble(where_to, local, pieces):
    size = pieces[0].shape[0]
    count = len(pieces)

    def kernel(where_ref, local_ref, *refs):
        out_ref, held, read, written = refs[count:]
        starts = [pl.multiple_of(where_ref[i + 1], size) for i in range(count)]

        def inward(i, of_local):
            source = local_ref.at[pl.ds(starts[i], size)] if of_local else refs[i]
            return pltpu.make_async_copy(source, held.at[i], read.at[i])

        def outward(i):
            return pltpu.make_async_copy(held.at[i], out_ref.at[pl.ds(starts[i], size)], written.at[i])

        for of_local in (True, False):

            @pl.when(where_ref[0] == (1 if of_local else 0))
            def _():
                for i in range(count):
                    inward(i, of_local).start()
                for i in range(count):
                    inward(i, of_local).wait()
                    outward(i).start()

        for i in range(count):
            outward(i).wait()

    return pl.pallas_call(
        kernel,
        out_shape=jax.ShapeDtypeStruct(local.shape, local.dtype),
        in_specs=[pl.BlockSpec(memory_space=pltpu.SMEM)] + [pl.BlockSpec(memory_space=pl.ANY)] * (count + 1),
        out_specs=pl.BlockSpec(memory_space=pl.ANY),
        scratch_shapes=[
            pltpu.VMEM((count,) + pieces[0].shape, local.dtype),
            pltpu.SemaphoreType.DMA((count,)),
            pltpu.SemaphoreType.DMA((count,)),
        ],
        name="assemble",
    )(where_to, local, *pieces)


def make(n_grp, n_tile, n_arch):
    n_half, n_x = n_grp // 2, n_arch // 2
    ring = folded(n_half)

    def half_of(g):
        return g // n_half

    def far(g):
        return (g + n_half) % n_grp

    def home(g, a):
        return a % 2 == half_of(g)

    def number(g, t, a):
        return (g * n_tile + t) * n_arch + a

    def send(x, to):
        pairs = []
        for g in range(n_grp):
            for t in range(n_tile):
                for a in range(n_arch):
                    other = to(g, t, a)
                    if other is not None:
                        pairs.append((number(g, t, a), number(*other)))
        return lax.ppermute(x, ("grp", "tile", "arch"), pairs)

    def cross(x):
        return send(x, lambda g, t, a: None if home(g, a) else (far(g), t, a ^ 1))

    def core(x):
        return send(x, lambda g, t, a: (g, t, a ^ 1))

    def onward(x, only=None):
        def to(g, t, a):
            if only is not None and home(g, a) != only:
                return None
            after = ring[(ring.index(g % n_half) + 1) % n_half]
            return (half_of(g) * n_half + after, t, a)

        return send(x, to)

    def to_tile(x, k, only=None):
        return send(x, lambda g, t, a: (g, (t + k) % n_tile, a) if only is None or home(g, a) == only else None)

    def to_x(x, k):
        return send(x, lambda g, t, a: None if home(g, a) else (g, t, (a + 2 * k) % n_arch))

    def to_arch(x, k):
        return send(x, lambda g, t, a: (g, t, (a + k) % n_arch))

    def to_grp(x, k):
        return send(x, lambda g, t, a: ((g + k) % n_grp, t, a))

    def to_away(x):
        return send(x, lambda g, t, a: (far(g), t, a) if home(g, a) else None)

    def per_device(query_grads, input_basis, output_basis, eigenvalues, activations, gradients, seq_lengths):
        query = query_grads[0]
        nf, nd = query.shape
        width = nd // n_tile
        rows = activations.shape[0]
        grp, tile, arch = lax.axis_index("grp"), lax.axis_index("tile"), lax.axis_index("arch")
        mine = arch % 2
        plane_half = grp // n_half
        at_home = mine == plane_half
        order = jnp.asarray(ring, jnp.int32)
        pos = jnp.asarray([ring.index(i) for i in range(n_half)], jnp.int32)[grp % n_half]
        own_base = mine * n_half
        other_base = n_half - own_base

        def at(k):
            return order[(pos + k) % n_half]

        parts = n_tile * n_x
        part = input_basis.shape[0] // parts
        piece = part // 2
        place_t, place_x = tile, arch // 2
        pieces = []
        for e in range(2):
            start = (place_t * n_x + place_x) * part + e * piece
            own = lax.optimization_barrier(rows_at(input_basis, start, piece))
            own = to_away(own)
            if e == 0:
                held = [(0, 0, own)]
                held += [(k, 0, to_tile(own, k, False)) for k in range(1, n_tile)]
                held += [(kt, k, to_x(one, k)) for k in range(1, n_x) for kt, _, one in list(held)]
            else:
                held = [(0, 0, own)]
                held += [(0, k, to_x(own, k)) for k in range(1, n_x)]
                held += [(k, kx, to_tile(one, k, False)) for k in range(1, n_tile) for _, kx, one in list(held)]
            pieces += [(kt, kx, e, one) for kt, kx, one in held]
        starts = [
            (((place_t - kt) % n_tile) * n_x + (place_x - kx) % n_x) * part + e * piece
            for kt, kx, e, _ in pieces
        ]
        where_to = jnp.stack([at_home.astype(jnp.int32)] + [one.astype(jnp.int32) for one in starts])
        basis = assemble(where_to, input_basis, [one for _, _, _, one in pieces])

        half = nf // 2
        sums = []
        for e in range(2):
            held = query[e * half : (e + 1) * half]
            held = jnp.where(at_home, held, cross(held))
            total = 0.0
            for s in range(n_half):
                if s:
                    held = onward(held)
                theirs = core(held)
                total += mm(held, rows_at(basis, (own_base + at(-s)) * nd, nd))
                total += mm(theirs, rows_at(basis, (other_base + at(-s)) * nd, nd))
            sums.append(total.astype(bf16))
        rotated_in = jnp.concatenate(sums, axis=0)

        bases = [output_basis]
        hv = output_basis.shape[0] // 2
        for k in range(1, n_tile):
            one = to_tile(rows_at(output_basis, mine * hv, hv), k)
            two = core(one)
            whole = jnp.zeros_like(output_basis)
            whole = lax.dynamic_update_slice_in_dim(whole, one, mine * hv, 0)
            bases.append(lax.dynamic_update_slice_in_dim(whole, two, (1 - mine) * hv, 0))
        factor = (1.0 / (eigenvalues + damping)).astype(bf16)
        factors = [cols_at(factor, tile * width, width)]
        for k in range(1, n_tile):
            one = cols_at(factor, ((tile + k) % n_tile) * width, width)
            factors.append(to_tile(one, k, True))
        factors = jnp.concatenate(factors, axis=0)
        portion = factors.shape[0] // n_x
        place = arch // 2
        one = to_away(rows_at(factors, place * portion, portion))
        away = lax.dynamic_update_slice_in_dim(jnp.zeros_like(factors), one, place * portion, 0)
        for k in range(1, n_x):
            away = lax.dynamic_update_slice_in_dim(away, to_x(one, k), ((place - k) % n_x) * portion, 0)
        factors = jnp.where(at_home, factors, away)
        factors = [factors[k * nf : (k + 1) * nf] for k in range(n_tile)]
        both = jnp.concatenate([activations, gradients], axis=1)
        both = [both] + [to_arch(both, k) for k in range(1, n_arch)]
        both = jnp.concatenate(both, axis=0)

        parts = [cols_at(rotated_in, tile * width, width)]
        for k in range(1, n_tile):
            one = cols_at(rotated_in, ((tile + k) % n_tile) * width, width)
            parts.append(to_tile(one, k))
        scaled = []
        for one_basis, one_factor in zip(bases, factors):
            rotated = 0.0
            for k, one in enumerate(parts):
                rotated += mm_tn(rows_at(one_basis, ((tile - k) % n_tile) * nf, nf), one)
            scaled.append((rotated * one_factor.astype(f32)).astype(bf16))
        restored = jnp.zeros((nd, nf), bf16)
        for k in range(n_tile):
            back = 0.0
            for one_basis, one in zip(bases, scaled):
                back += mm_tt(one, rows_at(one_basis, ((tile + k) % n_tile) * nf, nf))
            back = back.astype(bf16)
            if k:
                back = to_tile(back, k)
            restored = lax.dynamic_update_slice_in_dim(restored, back, ((tile - k) % n_tile) * width, 0)

        hd = nd // 2

        def product(block, e):
            return mm(rows_at(basis, block * nd + e * hd, hd), restored)

        outs = []
        for e in range(2):
            for s in range(1, n_half + 1):
                theirs = product(other_base + at(-s), e).astype(bf16)
                theirs = core(theirs)
                added = product(own_base + at(-s), e) + theirs.astype(f32)
                if s > 1:
                    added = lax.optimization_barrier(added)
                    away_total = (added + onward(away_total, False).astype(f32)).astype(bf16)
                    home_total = (added + onward(home_total, True).astype(f32)).astype(bf16)
                else:
                    away_total = home_total = added.astype(bf16)
            outs.append(jnp.where(at_home, home_total, cross(away_total)))
        preconditioned = jnp.concatenate(outs, axis=0)
        all_acts, all_grads = both[:, :nd], both[:, nd:]

        projected = mm(all_acts, preconditioned)
        tokens = jnp.sum(projected * all_grads.astype(f32), axis=1).reshape(n_arch, rows)
        token_parts = [tokens[0]]
        for k in range(1, n_arch):
            token_parts.append(to_arch(tokens[k], n_arch - k))
        lengths = seq_lengths[0]
        ends = jnp.cumsum(lengths)
        starts = ends - lengths
        position = jnp.arange(rows, dtype=jnp.int32)
        member = ((position[None, :] >= starts[:, None]) & (position[None, :] < ends[:, None])).astype(f32)
        totals = [jnp.dot(one[None], member.T, precision=lax.Precision.HIGHEST) for one in token_parts]
        totals = jnp.concatenate(totals, axis=0)
        totals = sum([to_tile(totals, k) for k in range(1, n_tile)], totals)
        totals = sum([to_grp(totals, k) for k in range(1, n_grp)], totals)
        scores = totals / lengths.astype(f32)[None, :]
        return preconditioned[None], jnp.roll(scores, arch, axis=0)

    return per_device


def solution(mesh):
    n_grp, n_tile, n_arch = mesh.shape["grp"], mesh.shape["tile"], mesh.shape["arch"]
    return jax.shard_map(
        make(n_grp, n_tile, n_arch),
        mesh=mesh,
        in_specs=(
            P("arch", "tile", "grp"),
            P(None, "grp"),
            P(None, "tile"),
            P("tile", "grp"),
            P("arch", "grp"),
            P("arch", "tile"),
            P("arch", None),
        ),
        out_specs=(P("arch", "grp", "tile"), P(None, "arch")),
        check_vma=False,
    )
```

time: 337 us -> 322 us (0.955)
  waiting for transfers between devices: 217 us -> 83.6 us
  starting transfers between devices: 42.8 us -> 143 us
  local copies, waits for them, and re-layouts: 5.47 us -> 24.4 us
  other arithmetic: 2.98 us -> 17.9 us
  matrix products: 56.9 us -> 42.9 us
  between operations: 11.4 us -> 1.27 us
  Pallas kernels: 0 us -> 7.16 us
    ppermute x29 -> x43, waiting for transfers between devices: 217 us -> 83.6 us  [send(): return lax.ppermute(x, ('grp', 'tile', 'arch'), pairs)]
    ppermute x29 -> x43, starting transfers between devices: 42.8 us -> 143 us  [send(): return lax.ppermute(x, ('grp', 'tile', 'arch'), pairs)]
    dot_general x9 -> x8, matrix products: 22.5 us -> 6.36 us  [the longest x4 5.88 us: mm_tt(): lax.dot_general(a, b, (((0,), (1,)), ((), ())), preferred_element_type=f32)]
    pallas_call x0 -> x1, Pallas kernels: none -> 7.16 us  [assemble(): pl.pallas_call(kernel, out_shape=jax.ShapeDtypeStruct(local.shape, local....]
    concatenate x1 -> x6, other arithmetic: 0.96 us -> 7.71 us  [the longest x1 4.67 us: per_device(): both = jnp.concatenate(both, axis=0)]
    dynamic_update_slice x1 -> x5, local copies, waits for them, and re-layouts: 0.1 us -> 6.7 us  [the longest x1 2.42 us: per_device(): whole = lax.dynamic_update_slice_in_dim(whole, one, mine * hv, 0)]
    dot_general x13 -> x17, matrix products: 25.1 us -> 30.7 us  [mm(): lax.dot_general(a, b, (((1,), (0,)), ((), ())), preferred_element_type=f32)]
    select_n x0 -> x4, other arithmetic: none -> 4.79 us  [the longest x1 2.73 us: per_device(): held = jnp.where(at_home, held, cross(held))]
  transfers between devices with their start and end apart: 29 -> 43, of which waited for: 24 -> 15; matrix products, arithmetic and copies ran while one was open for 15% -> 24% of each run, Pallas kernels for 0% -> 2%
where the time goes in v2:
time: 322 us; the launch traced here: 320 us
  starting transfers between devices  143 us (44%)
  waiting for transfers between devices  83.6 us (26%)
  matrix products  42.9 us (13%)
  local copies, waits for them, and re-layouts  24.4 us (8%)
  other arithmetic  17.9 us (6%)
  Pallas kernels  7.16 us (2%)
    ppermute x43, starting transfers between devices, send(): return lax.ppermute(x, ('grp', 'tile', 'arch'), pairs)  143 us
    ppermute x43, waiting for transfers between devices, send(): return lax.ppermute(x, ('grp', 'tile', 'arch'), pairs)  83.6 us
    dot_general x17, matrix products, mm(): lax.dot_general(a, b, (((1,), (0,)), ((), ())), preferred_element_type=f32)  30.7 us
    pallas_call x1, Pallas kernels, assemble(): pl.pallas_call(kernel, out_shape=jax.ShapeDtypeStruct(local.shape, local....  7.16 us
  transfers between devices with their start and end apart: 43, of which 15 were waited for; matrix products, arithmetic and copies ran while one was open for 24% of the time, Pallas kernels for 2%

profile of v2, /device:TPU:0, one launch (start us, length us, event | category | flops | bytes accessed | tf_op | source)
XLA Modules:
  0.0 320.2 jit_solution(9591591498121808924)
XLA Ops:
  0.6 2.8 slice_bitcast_fusion
  3.4 1.6 collective-permute-start.12
  5.0 3.1 constant_dynamic-slice_fusion.4
  8.1 7.3 %collective-permute-start = (bf16[512,1024]{1,0:T(8,128)(2,1)}, bf16[512,1024]{1,0:T(8,128)(2,1)}, u32[]{:S(2)}, u32[]{:S(2)}) collective-permute-start(bf16[512,1024]{1,0:T(8,128)(2,1)} %get-tuple-element.3), channel_id=1, source_target_pairs={{0,16},{2,18},{4,20},{6,22},{8,24},{10,26},{12,28},{14,30},{17,1},... | collective-permute-start | bytes 3145736 | tf_op jit(solution)/shard_map/ppermute | solution.py:103
  15.4 2.3 collective-permute-start.4
  17.7 1.6 collective-permute-start.8
  20.4 1.5 collective-permute-start.20
  21.9 3.5 %divide_convert_fusion = bf16[768,1024]{1,0:T(8,128)(2,1)} fusion(f32[768,1024]{1,0:T(8,128)} %param.12), kind=kLoop, calls=%fused_computation.2 | loop fusion | flops 2359296 | bytes 4718592 | tf_op jit(solution)/shard_map/convert_element_type | solution.py:200
  25.4 2.4 constant_dynamic-slice_fusion.2
  27.8 2.4 collective-permute-start.17
  30.2 2.7 broadcast_select_fusion
  33.0 1.6 collective-permute-start.14
  34.5 3.7 %collective-permute-done.refs_0_ = bf16[512,1024]{1,0:T(8,128)(2,1)} collective-permute-done((bf16[512,1024]{1,0:T(8,128)(2,1)}, bf16[512,1024]{1,0:T(8,128)(2,1)}, u32[]{:S(2)}, u32[]{:S(2)}) %collective-permute-start) | collective-permute-done | bytes 1048608 | tf_op jit(solution)/shard_map/ppermute | solution.py:103
  38.3 1.6 collective-permute-start.1
  39.9 9.7 %collective-permute-done.4.refs_4_ = bf16[512,1024]{1,0:T(8,128)(2,1)} collective-permute-done((bf16[512,1024]{1,0:T(8,128)(2,1)}, bf16[512,1024]{1,0:T(8,128)(2,1)}, u32[]{:S(2)}, u32[]{:S(2)}) %collective-permute-start.4) | collective-permute-done | bytes 1048608 | tf_op jit(solution)/shard_map/ppermute | solution.py:103
  49.6 1.6 collective-permute-start.5
  51.2 3.7 %collective-permute-done.17 = bf16[768,512]{1,0:T(8,128)(2,1)} collective-permute-done((bf16[768,512]{1,0:T(8,128)(2,1)}, bf16[768,512]{1,0:T(8,128)(2,1)}, u32[]{:S(2)}, u32[]{:S(2)}) %collective-permute-start.17) | collective-permute-done | bytes 786464 | tf_op jit(solution)/shard_map/ppermute | solution.py:103
  54.9 37.1 %collective-permute-start.10 = (bf16[384,1024]{1,0:T(8,128)(2,1)}, bf16[384,1024]{1,0:T(8,128)(2,1)}, u32[]{:S(2)}, u32[]{:S(2)}) collective-permute-start(bf16[384,1024]{1,0:T(8,128)(2,1)} %get-tuple-element.7), channel_id=1, source_target_pairs={{0,8},{1,9},{2,10},{3,11},{4,12},{5,13},{6,14},{7,15},{8,0},{9,1},... | collective-permute-start | bytes 2359304 | tf_op jit(solution)/shard_map/ppermute | solution.py:103
  92.9 8.1 %collective-permute-start.18 = (bf16[768,512]{1,0:T(8,128)(2,1)S(1)}, bf16[768,512]{1,0:T(8,128)(2,1)S(1)}, u32[]{:S(2)}, u32[]{:S(2)}) collective-permute-start(bf16[768,512]{1,0:T(8,128)(2,1)S(1)} %fusion.50), channel_id=1, source_target_pairs={{0,16},{2,18},{4,20},{6,22},{8,24},{10,26},{12,28},{14,30},{17,1},... | collective-permute-start | bytes 2359304 | tf_op jit(solution)/shard_map/ppermute | solution.py:103
  101.0 10.3 %collective-permute-start.21 = (bf16[768,768]{1,0:T(8,128)(2,1)}, bf16[768,768]{1,0:T(8,128)(2,1)}, u32[]{:S(2)}, u32[]{:S(2)}) collective-permute-start(bf16[768,768]{1,0:T(8,128)(2,1)} %collective-permute-done.20), channel_id=1, source_target_pairs={{0,1},{1,0},{2,3},{3,2},{4,5},{5,4},{6,7},{7,6},{8,9},{9,8},{10,11... | collective-permute-start | bytes 3538952 | tf_op jit(solution)/shard_map/ppermute | solution.py:103
  111.3 7.7 %collective-permute-done.10 = bf16[384,1024]{1,0:T(8,128)(2,1)} collective-permute-done((bf16[384,1024]{1,0:T(8,128)(2,1)}, bf16[384,1024]{1,0:T(8,128)(2,1)}, u32[]{:S(2)}, u32[]{:S(2)}) %collective-permute-start.10) | collective-permute-done | bytes 786464 | tf_op jit(solution)/shard_map/ppermute | solution.py:103
  119.1 1.6 collective-permute-start.2
  122.9 1.7 collective-permute-start.6
  124.6 1.6 collective-permute-start.3
  126.2 1.7 collective-permute-start.7
  127.9 2.1 copy.11
  132.0 2.0 pad_maximum_fusion.4
  134.0 1.6 broadcast_in_dim.10
  135.6 2.4 constant_dynamic-update-slice_fusion.2
  138.0 7.4 %collective-permute-start.13 = (bf16[384,1024]{1,0:T(8,128)(2,1)}, bf16[384,1024]{1,0:T(8,128)(2,1)}, u32[]{:S(2)}, u32[]{:S(2)}) collective-permute-start(bf16[384,1024]{1,0:T(8,128)(2,1)} %get-tuple-element.6), channel_id=1, source_target_pairs={{0,1},{1,0},{2,3},{3,2},{4,5},{5,4},{6,7},{7,6},{8,9},{9,8},{10,11... | collective-permute-start | bytes 2359304 | tf_op jit(solution)/shard_map/ppermute | solution.py:103
  147.6 2.4 constant_dynamic-update-slice_fusion.1
  150.0 1.6 collective-permute-start.9
  151.6 3.2 %collective-permute-start.11 = (bf16[384,1024]{1,0:T(8,128)(2,1)}, bf16[384,1024]{1,0:T(8,128)(2,1)}, u32[]{:S(2)}, u32[]{:S(2)}) collective-permute-start(bf16[384,1024]{1,0:T(8,128)(2,1)} %collective-permute-done.10), channel_id=1, source_target_pairs={{0,1},{1,0},{2,3},{3,2},{4,5},{5,4},{6,7},{7,6},{8,9},{9,8},{10,11... | collective-permute-start | bytes 2359304 | tf_op jit(solution)/shard_map/ppermute | solution.py:103
  154.9 7.2 %assemble.1 = bf16[4096,1024]{1,0:T(8,128)(2,1)} custom-call(s32[9]{0:T(128)} %stack.43.where_ref, bf16[4096,1024]{1,0:T(8,128)(2,1)} %local_ref.1, bf16[512,1024]{1,0:T(8,128)(2,1)} %collective-permute-done.refs_0_, bf16[512,1024]{1,0:T(8,128)(2,1)} %collective-permute-done.1.refs_1_, bf16[512,1024]{1,0:T(8,128)(2,1)} %collective-permute-done.2.refs_2_, ...), custom_call_target="tpu_custom_call" | custom-call | tf_op jit(solution)/shard_map/assemble/pallas_call | solution.py:65
  162.0 3.0 fusion.6
  165.0 3.1 fusion.8
  169.1 2.1 fusion.10
  171.2 2.1 fusion.12
  173.4 2.1 fusion.2
  175.5 2.2 add_convert_fusion.8
  177.7 2.1 fusion.4
  179.9 2.3 add_convert_fusion.9
  182.2 1.5 collective-permute-start.16
  184.7 1.6 fusion.18
  187.1 15.1 %collective-permute-done.16 = bf16[768,512]{1,0:T(8,128)(2,1)S(1)} collective-permute-done((bf16[768,512]{1,0:T(8,128)(2,1)S(1)}, bf16[768,512]{1,0:T(8,128)(2,1)S(1)}, u32[]{:S(2)}, u32[]{:S(2)}) %collective-permute-start.16) | collective-permute-done | bytes 786464 | tf_op jit(solution)/shard_map/ppermute | solution.py:103
  202.2 2.1 fusion.29
  204.3 2.1 multiply_convert_fusion
  208.1 2.1 add_convert_fusion.6
  210.2 1.5 collective-permute-start.22
  212.7 2.1 fusion.23
  214.9 15.2 %collective-permute-done.22 = bf16[512,768]{1,0:T(8,128)(2,1)S(1)} collective-permute-done((bf16[512,768]{1,0:T(8,128)(2,1)S(1)}, bf16[512,768]{1,0:T(8,128)(2,1)S(1)}, u32[]{:S(2)}, u32[]{:S(2)}) %collective-permute-start.22) | collective-permute-done | bytes 786464 | tf_op jit(solution)/shard_map/ppermute | solution.py:103
  240.2 9.1 %collective-permute-start.35 = (bf16[256,1792]{0,1:T(8,128)(2,1)}, bf16[256,1792]{0,1:T(8,128)(2,1)S(1)}, u32[]{:S(2)}, u32[]{:S(2)}) collective-permute-start(bf16[256,1792]{0,1:T(8,128)(2,1)} %pad_maximum_fusion.4), channel_id=1, source_target_pairs={{0,3},{1,0},{2,1},{3,2},{4,7},{5,4},{6,5},{7,6},{8,11},{9,8},{10,9... | collective-permute-start | bytes 2752520 | tf_op jit(solution)/shard_map/ppermute | solution.py:103
  249.5 3.3 %collective-permute-start.25 = (bf16[512,768]{1,0:T(8,128)(2,1)S(1)}, bf16[512,768]{1,0:T(8,128)(2,1)S(1)}, u32[]{:S(2)}, u32[]{:S(2)}) collective-permute-start(bf16[512,768]{1,0:T(8,128)(2,1)S(1)} %add_convert_fusion.5), channel_id=1, source_target_pairs={{0,8},{2,10},{4,12},{6,14},{8,0},{10,2},{12,4},{14,6},{17,25},{19,... | collective-permute-start | bytes 2359304 | tf_op jit(solution)/shard_map/ppermute | solution.py:103
  254.8 2.5 collective-permute-start.30
  257.3 2.4 collective-permute-done.34
  260.4 9.7 %collective-permute-done.35 = bf16[256,1792]{0,1:T(8,128)(2,1)S(1)} collective-permute-done((bf16[256,1792]{0,1:T(8,128)(2,1)}, bf16[256,1792]{0,1:T(8,128)(2,1)S(1)}, u32[]{:S(2)}, u32[]{:S(2)}) %collective-permute-start.35) | collective-permute-done | bytes 917536 | tf_op jit(solution)/shard_map/ppermute | solution.py:103
  270.1 4.7 %pad_maximum_fusion = bf16[1024,1792]{0,1:T(8,128)(2,1)S(1)} fusion(bf16[256,1792]{0,1:T(8,128)(2,1)S(1)} %collective-permute-done.35, bf16[256,1792]{0,1:T(8,128)(2,1)S(1)} %collective-permute-done.34, bf16[256,1792]{0,1:T(8,128)(2,1)} %collective-permute-done.33, bf16[256,768]{0,1:T(8,128)(2,1)S(1)} %copy.12, bf16[256,1024]{0,1:T(8,128)(2,1)S(1)} %copy-done.2), kind=kLoop, calls=%fused_computation | loop fusion | flops 18350080 | bytes 7340032 | tf_op jit(solution)/shard_map/concatenate | solution.py:216
  275.0 8.8 %collective-permute-done.30 = bf16[512,768]{1,0:T(8,128)(2,1)S(1)} collective-permute-done((bf16[512,768]{1,0:T(8,128)(2,1)S(1)}, bf16[512,768]{1,0:T(8,128)(2,1)S(1)}, u32[]{:S(2)}, u32[]{:S(2)}) %collective-permute-start.30) | collective-permute-done | bytes 786464 | tf_op jit(solution)/shard_map/ppermute | solution.py:103
  284.1 3.4 %multiply_reduce_fusion = f32[1024]{0:T(1024)S(1)} fusion(bf16[256,1792]{0,1:T(8,128)(2,1)S(1)} %collective-permute-done.35, bf16[256,1792]{0,1:T(8,128)(2,1)S(1)} %collective-permute-done.34, bf16[256,1792]{0,1:T(8,128)(2,1)} %collective-permute-done.33, bf16[256,768]{0,1:T(8,128)(2,1)S(1)} %copy.12, bf16[256,1024]{0,1:T(8,128)(2,1)S(1)} %copy-done.2, ...), kind=kOutput, calls=%fused_computation.1 | convolution fusion | flops 1623194624 | bytes 7344128 | tf_op jit(solution)/shard_map/dot_general | solution.py:14
  287.5 15.7 %collective-permute-start.36 = (f32[256]{0:T(256)S(1)}, f32[256]{0:T(256)S(1)}, u32[]{:S(2)}, u32[]{:S(2)}) collective-permute-start(f32[256]{0:T(256)S(1)} %get-tuple-element.13), channel_id=1, source_target_pairs={{0,3},{1,0},{2,1},{3,2},{4,7},{5,4},{6,5},{7,6},{8,11},{9,8},{10,9... | collective-permute-start | bytes 3080 | tf_op jit(solution)/shard_map/ppermute | solution.py:103
  303.2 2.8 collective-permute-start.37
  309.2 1.5 collective-permute-start.39
  313.6 2.4 collective-permute-start.41
  316.7 1.6 collective-permute-done.40
  (103 shorter events, 35.9 us)
Async XLA Ops:
  0.6 18.7 %copy-start = (bf16[1536,768]{1,0:T(8,128)(2,1)S(1)}, bf16[1536,768]{1,0:T(8,128)(2,1)}, u32[]{:S(2)}) copy-start(bf16[1536,768]{1,0:T(8,128)(2,1)} %param.11) | copy-start | bytes 7077892
  3.4 24.4 %collective-permute-start.12 = (bf16[384,1024]{1,0:T(8,128)(2,1)}, bf16[384,1024]{1,0:T(8,128)(2,1)}, u32[]{:S(2)}, u32[]{:S(2)}) collective-permute-start(bf16[384,1024]{1,0:T(8,128)(2,1)} %get-tuple-element.8), channel_id=1, source_target_pairs={{1,16},{3,18},{5,20},{7,22},{9,24},{11,26},{13,28},{15,30},{16,1},... | collective-permute-start | bytes 2359304 | tf_op jit(solution)/shard_map/ppermute | solution.py:103
  8.1 30.2 %collective-permute-start = (bf16[512,1024]{1,0:T(8,128)(2,1)}, bf16[512,1024]{1,0:T(8,128)(2,1)}, u32[]{:S(2)}, u32[]{:S(2)}) collective-permute-start(bf16[512,1024]{1,0:T(8,128)(2,1)} %get-tuple-element.3), channel_id=1, source_target_pairs={{0,16},{2,18},{4,20},{6,22},{8,24},{10,26},{12,28},{14,30},{17,1},... | collective-permute-start | bytes 3145736 | tf_op jit(solution)/shard_map/ppermute | solution.py:103
  15.4 34.2 %collective-permute-start.4 = (bf16[512,1024]{1,0:T(8,128)(2,1)}, bf16[512,1024]{1,0:T(8,128)(2,1)}, u32[]{:S(2)}, u32[]{:S(2)}) collective-permute-start(bf16[512,1024]{1,0:T(8,128)(2,1)} %get-tuple-element.2), channel_id=1, source_target_pairs={{0,16},{2,18},{4,20},{6,22},{8,24},{10,26},{12,28},{14,30},{17,1},... | collective-permute-start | bytes 3145736 | tf_op jit(solution)/shard_map/ppermute | solution.py:103
  17.7 12.5 %collective-permute-start.8 = (bf16[384,1024]{1,0:T(8,128)(2,1)}, bf16[384,1024]{1,0:T(8,128)(2,1)}, u32[]{:S(2)}, u32[]{:S(2)}) collective-permute-start(bf16[384,1024]{1,0:T(8,128)(2,1)} %get-tuple-element.9), channel_id=1, source_target_pairs={{1,16},{3,18},{5,20},{7,22},{9,24},{11,26},{13,28},{15,30},{16,1},... | collective-permute-start | bytes 2359304 | tf_op jit(solution)/shard_map/ppermute | solution.py:103
  20.4 72.5 %collective-permute-start.20 = (bf16[768,768]{1,0:T(8,128)(2,1)}, bf16[768,768]{1,0:T(8,128)(2,1)}, u32[]{:S(2)}, u32[]{:S(2)}) collective-permute-start(bf16[768,768]{1,0:T(8,128)(2,1)} %constant_dynamic-slice_fusion.1), channel_id=1, source_target_pairs={{0,4},{1,5},{2,6},{3,7},{4,0},{5,1},{6,2},{7,3},{8,12},{9,13},{10,... | collective-permute-start | bytes 3538952 | tf_op jit(solution)/shard_map/ppermute | solution.py:103
  27.8 27.1 %collective-permute-start.17 = (bf16[768,512]{1,0:T(8,128)(2,1)}, bf16[768,512]{1,0:T(8,128)(2,1)}, u32[]{:S(2)}, u32[]{:S(2)}) collective-permute-start(bf16[768,512]{1,0:T(8,128)(2,1)} %get-tuple-element.4), channel_id=1, source_target_pairs={{0,4},{2,6},{4,0},{6,2},{8,12},{10,14},{12,8},{14,10},{17,21},{19,... | collective-permute-start | bytes 2359304 | tf_op jit(solution)/shard_map/ppermute | solution.py:103
  33.0 68.1 %collective-permute-start.14 = (bf16[384,1024]{1,0:T(8,128)(2,1)}, bf16[384,1024]{1,0:T(8,128)(2,1)}, u32[]{:S(2)}, u32[]{:S(2)}) collective-permute-start(bf16[384,1024]{1,0:T(8,128)(2,1)} %get-tuple-element.6), channel_id=1, source_target_pairs={{0,8},{1,9},{2,10},{3,11},{4,12},{5,13},{6,14},{7,15},{8,0},{9,1},... | collective-permute-start | bytes 2359304 | tf_op jit(solution)/shard_map/ppermute | solution.py:103
  38.3 86.3 %collective-permute-start.1 = (bf16[512,1024]{1,0:T(8,128)(2,1)}, bf16[512,1024]{1,0:T(8,128)(2,1)}, u32[]{:S(2)}, u32[]{:S(2)}) collective-permute-start(bf16[512,1024]{1,0:T(8,128)(2,1)} %collective-permute-done.refs_0_), channel_id=1, source_target_pairs={{1,5},{3,7},{5,1},{7,3},{9,13},{11,15},{13,9},{15,11},{16,20},{18,... | collective-permute-start | bytes 3145736 | tf_op jit(solution)/shard_map/ppermute | solution.py:103
  49.6 76.6 %collective-permute-start.5 = (bf16[512,1024]{1,0:T(8,128)(2,1)}, bf16[512,1024]{1,0:T(8,128)(2,1)}, u32[]{:S(2)}, u32[]{:S(2)}) collective-permute-start(bf16[512,1024]{1,0:T(8,128)(2,1)} %collective-permute-done.4.refs_4_), channel_id=1, source_target_pairs={{1,3},{3,1},{5,7},{7,5},{9,11},{11,9},{13,15},{15,13},{16,18},{18,... | collective-permute-start | bytes 3145736 | tf_op jit(solution)/shard_map/ppermute | solution.py:103
  54.9 64.2 %collective-permute-start.10 = (bf16[384,1024]{1,0:T(8,128)(2,1)}, bf16[384,1024]{1,0:T(8,128)(2,1)}, u32[]{:S(2)}, u32[]{:S(2)}) collective-permute-start(bf16[384,1024]{1,0:T(8,128)(2,1)} %get-tuple-element.7), channel_id=1, source_target_pairs={{0,8},{1,9},{2,10},{3,11},{4,12},{5,13},{6,14},{7,15},{8,0},{9,1},... | collective-permute-start | bytes 2359304 | tf_op jit(solution)/shard_map/ppermute | solution.py:103
  92.9 38.2 %copy-start.6 = (s32[1,8]{1,0:T(1,128)S(1)}, s32[1,8]{1,0:T(1,128)}, u32[]{:S(2)}) copy-start(s32[1,8]{1,0:T(1,128)} %param.15) | copy-start | bytes 100
  92.9 29.0 %collective-permute-start.18 = (bf16[768,512]{1,0:T(8,128)(2,1)S(1)}, bf16[768,512]{1,0:T(8,128)(2,1)S(1)}, u32[]{:S(2)}, u32[]{:S(2)}) collective-permute-start(bf16[768,512]{1,0:T(8,128)(2,1)S(1)} %fusion.50), channel_id=1, source_target_pairs={{0,16},{2,18},{4,20},{6,22},{8,24},{10,26},{12,28},{14,30},{17,1},... | collective-permute-start | bytes 2359304 | tf_op jit(solution)/shard_map/ppermute | solution.py:103
  101.0 37.0 %collective-permute-start.21 = (bf16[768,768]{1,0:T(8,128)(2,1)}, bf16[768,768]{1,0:T(8,128)(2,1)}, u32[]{:S(2)}, u32[]{:S(2)}) collective-permute-start(bf16[768,768]{1,0:T(8,128)(2,1)} %collective-permute-done.20), channel_id=1, source_target_pairs={{0,1},{1,0},{2,3},{3,2},{4,5},{5,4},{6,7},{7,6},{8,9},{9,8},{10,11... | collective-permute-start | bytes 3538952 | tf_op jit(solution)/shard_map/ppermute | solution.py:103
  119.1 30.9 %collective-permute-start.2 = (bf16[512,1024]{1,0:T(8,128)(2,1)}, bf16[512,1024]{1,0:T(8,128)(2,1)}, u32[]{:S(2)}, u32[]{:S(2)}) collective-permute-start(bf16[512,1024]{1,0:T(8,128)(2,1)} %collective-permute-done.refs_0_), channel_id=1, source_target_pairs={{1,3},{3,1},{5,7},{7,5},{9,11},{11,9},{13,15},{15,13},{16,18},{18,... | collective-permute-start | bytes 3145736 | tf_op jit(solution)/shard_map/ppermute | solution.py:103
  121.9 0.9 copy-start.3
  122.9 27.1 %collective-permute-start.6 = (bf16[512,1024]{1,0:T(8,128)(2,1)}, bf16[512,1024]{1,0:T(8,128)(2,1)}, u32[]{:S(2)}, u32[]{:S(2)}) collective-permute-start(bf16[512,1024]{1,0:T(8,128)(2,1)} %collective-permute-done.4.refs_4_), channel_id=1, source_target_pairs={{1,5},{3,7},{5,1},{7,3},{9,13},{11,15},{13,9},{15,11},{16,20},{18,... | collective-permute-start | bytes 3145736 | tf_op jit(solution)/shard_map/ppermute | solution.py:103
  124.6 27.0 %collective-permute-start.3 = (bf16[512,1024]{1,0:T(8,128)(2,1)}, bf16[512,1024]{1,0:T(8,128)(2,1)}, u32[]{:S(2)}, u32[]{:S(2)}) collective-permute-start(bf16[512,1024]{1,0:T(8,128)(2,1)} %collective-permute-done.1.refs_1_), channel_id=1, source_target_pairs={{1,3},{3,1},{5,7},{7,5},{9,11},{11,9},{13,15},{15,13},{16,18},{18,... | collective-permute-start | bytes 3145736 | tf_op jit(solution)/shard_map/ppermute | solution.py:103
  126.2 25.4 %collective-permute-start.7 = (bf16[512,1024]{1,0:T(8,128)(2,1)}, bf16[512,1024]{1,0:T(8,128)(2,1)}, u32[]{:S(2)}, u32[]{:S(2)}) collective-permute-start(bf16[512,1024]{1,0:T(8,128)(2,1)} %collective-permute-done.5.refs_5_), channel_id=1, source_target_pairs={{1,5},{3,7},{5,1},{7,3},{9,13},{11,15},{13,9},{15,11},{16,20},{18,... | collective-permute-start | bytes 3145736 | tf_op jit(solution)/shard_map/ppermute | solution.py:103
  135.6 11.0 %copy-start.4 = (bf16[768,512]{1,0:T(8,128)(2,1)S(1)}, bf16[768,512]{1,0:T(8,128)(2,1)}, u32[]{:S(2)}) copy-start(bf16[768,512]{1,0:T(8,128)(2,1)} %copy-done.3) | copy-start | bytes 2359300
  138.0 30.1 %collective-permute-start.13 = (bf16[384,1024]{1,0:T(8,128)(2,1)}, bf16[384,1024]{1,0:T(8,128)(2,1)}, u32[]{:S(2)}, u32[]{:S(2)}) collective-permute-start(bf16[384,1024]{1,0:T(8,128)(2,1)} %get-tuple-element.6), channel_id=1, source_target_pairs={{0,1},{1,0},{2,3},{3,2},{4,5},{5,4},{6,7},{7,6},{8,9},{9,8},{10,11... | collective-permute-start | bytes 2359304 | tf_op jit(solution)/shard_map/ppermute | solution.py:103
  150.0 104.8 %collective-permute-start.33 = (bf16[256,1792]{0,1:T(8,128)(2,1)}, bf16[256,1792]{0,1:T(8,128)(2,1)}, u32[]{:S(2)}, u32[]{:S(2)}) collective-permute-start(bf16[256,1792]{0,1:T(8,128)(2,1)} %pad_maximum_fusion.4), channel_id=1, source_target_pairs={{0,1},{1,2},{2,3},{3,0},{4,5},{5,6},{6,7},{7,4},{8,9},{9,10},{10,1... | collective-permute-start | bytes 2752520 | tf_op jit(solution)/shard_map/ppermute | solution.py:103
  150.0 21.2 %collective-permute-start.9 = (bf16[384,1024]{1,0:T(8,128)(2,1)}, bf16[384,1024]{1,0:T(8,128)(2,1)}, u32[]{:S(2)}, u32[]{:S(2)}) collective-permute-start(bf16[384,1024]{1,0:T(8,128)(2,1)} %get-tuple-element.7), channel_id=1, source_target_pairs={{0,1},{1,0},{2,3},{3,2},{4,5},{5,4},{6,7},{7,6},{8,9},{9,8},{10,11... | collective-permute-start | bytes 2359304 | tf_op jit(solution)/shard_map/ppermute | solution.py:103
  151.6 21.8 %collective-permute-start.15 = (bf16[384,1024]{1,0:T(8,128)(2,1)}, bf16[384,1024]{1,0:T(8,128)(2,1)}, u32[]{:S(2)}, u32[]{:S(2)}) collective-permute-start(bf16[384,1024]{1,0:T(8,128)(2,1)} %collective-permute-done.14), channel_id=1, source_target_pairs={{0,1},{1,0},{2,3},{3,2},{4,5},{5,4},{6,7},{7,6},{8,9},{9,8},{10,11... | collective-permute-start | bytes 2359304 | tf_op jit(solution)/shard_map/ppermute | solution.py:103
  151.6 26.1 %collective-permute-start.11 = (bf16[384,1024]{1,0:T(8,128)(2,1)}, bf16[384,1024]{1,0:T(8,128)(2,1)}, u32[]{:S(2)}, u32[]{:S(2)}) collective-permute-start(bf16[384,1024]{1,0:T(8,128)(2,1)} %collective-permute-done.10), channel_id=1, source_target_pairs={{0,1},{1,0},{2,3},{3,2},{4,5},{5,4},{6,7},{7,6},{8,9},{9,8},{10,11... | collective-permute-start | bytes 2359304 | tf_op jit(solution)/shard_map/ppermute | solution.py:103
  162.0 7.0 %copy-start.1 = (bf16[4096,1024]{1,0:T(8,128)(2,1)S(1)}, bf16[4096,1024]{1,0:T(8,128)(2,1)}, u32[]{:S(2)}) copy-start(bf16[4096,1024]{1,0:T(8,128)(2,1)} %assemble.1) | copy-start | bytes 25165828
  165.0 3.1 copy-start.5
  168.1 15.7 %collective-permute-start.19 = (bf16[768,512]{1,0:T(8,128)(2,1)S(1)}, bf16[768,512]{1,0:T(8,128)(2,1)S(1)}, u32[]{:S(2)}, u32[]{:S(2)}) collective-permute-start(bf16[768,512]{1,0:T(8,128)(2,1)S(1)} %copy-done.5), channel_id=1, source_target_pairs={{1,3},{3,1},{5,7},{7,5},{9,11},{11,9},{13,15},{15,13},{16,18},{18,... | collective-permute-start | bytes 2359304 | tf_op jit(solution)/shard_map/ppermute | solution.py:103
  182.2 20.0 %collective-permute-start.16 = (bf16[768,512]{1,0:T(8,128)(2,1)S(1)}, bf16[768,512]{1,0:T(8,128)(2,1)S(1)}, u32[]{:S(2)}, u32[]{:S(2)}) collective-permute-start(bf16[768,512]{1,0:T(8,128)(2,1)S(1)} %fusion.51), channel_id=1, source_target_pairs={{0,4},{1,5},{2,6},{3,7},{4,0},{5,1},{6,2},{7,3},{8,12},{9,13},{10,... | collective-permute-start | bytes 2359304 | tf_op jit(solution)/shard_map/ppermute | solution.py:103
  210.2 19.8 %collective-permute-start.22 = (bf16[512,768]{1,0:T(8,128)(2,1)S(1)}, bf16[512,768]{1,0:T(8,128)(2,1)S(1)}, u32[]{:S(2)}, u32[]{:S(2)}) collective-permute-start(bf16[512,768]{1,0:T(8,128)(2,1)S(1)} %add_convert_fusion.6), channel_id=1, source_target_pairs={{0,4},{1,5},{2,6},{3,7},{4,0},{5,1},{6,2},{7,3},{8,12},{9,13},{10,... | collective-permute-start | bytes 2359304 | tf_op jit(solution)/shard_map/ppermute | solution.py:103
  231.1 4.5 %collective-permute-start.24 = (bf16[512,768]{1,0:T(8,128)(2,1)S(1)}, bf16[512,768]{1,0:T(8,128)(2,1)S(1)}, u32[]{:S(2)}, u32[]{:S(2)}) collective-permute-start(bf16[512,768]{1,0:T(8,128)(2,1)S(1)} %convolution_convert_fusion.2), channel_id=1, source_target_pairs={{0,1},{1,0},{2,3},{3,2},{4,5},{5,4},{6,7},{7,6},{8,9},{9,8},{10,11... | collective-permute-start | bytes 2359304 | tf_op jit(solution)/shard_map/ppermute | solution.py:103
  232.4 4.9 %collective-permute-start.29 = (bf16[512,768]{1,0:T(8,128)(2,1)S(1)}, bf16[512,768]{1,0:T(8,128)(2,1)S(1)}, u32[]{:S(2)}, u32[]{:S(2)}) collective-permute-start(bf16[512,768]{1,0:T(8,128)(2,1)S(1)} %convolution_convert_fusion), channel_id=1, source_target_pairs={{0,1},{1,0},{2,3},{3,2},{4,5},{5,4},{6,7},{7,6},{8,9},{9,8},{10,11... | collective-permute-start | bytes 2359304 | tf_op jit(solution)/shard_map/ppermute | solution.py:103
  234.0 5.1 %collective-permute-start.23 = (bf16[512,768]{1,0:T(8,128)(2,1)S(1)}, bf16[512,768]{1,0:T(8,128)(2,1)S(1)}, u32[]{:S(2)}, u32[]{:S(2)}) collective-permute-start(bf16[512,768]{1,0:T(8,128)(2,1)S(1)} %convolution_convert_fusion.3), channel_id=1, source_target_pairs={{0,1},{1,0},{2,3},{3,2},{4,5},{5,4},{6,7},{7,6},{8,9},{9,8},{10,11... | collective-permute-start | bytes 2359304 | tf_op jit(solution)/shard_map/ppermute | solution.py:103
  235.1 14.4 %collective-permute-start.28 = (bf16[512,768]{1,0:T(8,128)(2,1)S(1)}, bf16[512,768]{1,0:T(8,128)(2,1)S(1)}, u32[]{:S(2)}, u32[]{:S(2)}) collective-permute-start(bf16[512,768]{1,0:T(8,128)(2,1)S(1)} %convolution_convert_fusion.1), channel_id=1, source_target_pairs={{0,1},{1,0},{2,3},{3,2},{4,5},{5,4},{6,7},{7,6},{8,9},{9,8},{10,11... | collective-permute-start | bytes 2359304 | tf_op jit(solution)/shard_map/ppermute | solution.py:103
  236.6 3.6 %collective-permute-start.26 = (bf16[512,768]{1,0:T(8,128)(2,1)S(1)}, bf16[512,768]{1,0:T(8,128)(2,1)S(1)}, u32[]{:S(2)}, u32[]{:S(2)}) collective-permute-start(bf16[512,768]{1,0:T(8,128)(2,1)S(1)} %add_convert_fusion.5), channel_id=1, source_target_pairs={{1,9},{3,11},{5,13},{7,15},{9,1},{11,3},{13,5},{15,7},{16,24},{18,... | collective-permute-start | bytes 2359304 | tf_op jit(solution)/shard_map/ppermute | solution.py:103
  238.4 14.4 %collective-permute-start.31 = (bf16[512,768]{1,0:T(8,128)(2,1)S(1)}, bf16[512,768]{1,0:T(8,128)(2,1)S(1)}, u32[]{:S(2)}, u32[]{:S(2)}) collective-permute-start(bf16[512,768]{1,0:T(8,128)(2,1)S(1)} %add_convert_fusion.2), channel_id=1, source_target_pairs={{1,9},{3,11},{5,13},{7,15},{9,1},{11,3},{13,5},{15,7},{16,24},{18,... | collective-permute-start | bytes 2359304 | tf_op jit(solution)/shard_map/ppermute | solution.py:103
  239.1 20.6 %collective-permute-start.34 = (bf16[256,1792]{0,1:T(8,128)(2,1)}, bf16[256,1792]{0,1:T(8,128)(2,1)S(1)}, u32[]{:S(2)}, u32[]{:S(2)}) collective-permute-start(bf16[256,1792]{0,1:T(8,128)(2,1)} %pad_maximum_fusion.4), channel_id=1, source_target_pairs={{0,2},{1,3},{2,0},{3,1},{4,6},{5,7},{6,4},{7,5},{8,10},{9,11},{10,... | collective-permute-start | bytes 2752520 | tf_op jit(solution)/shard_map/ppermute | solution.py:103
  240.2 29.9 %collective-permute-start.35 = (bf16[256,1792]{0,1:T(8,128)(2,1)}, bf16[256,1792]{0,1:T(8,128)(2,1)S(1)}, u32[]{:S(2)}, u32[]{:S(2)}) collective-permute-start(bf16[256,1792]{0,1:T(8,128)(2,1)} %pad_maximum_fusion.4), channel_id=1, source_target_pairs={{0,3},{1,0},{2,1},{3,2},{4,7},{5,4},{6,5},{7,6},{8,11},{9,8},{10,9... | collective-permute-start | bytes 2752520 | tf_op jit(solution)/shard_map/ppermute | solution.py:103
  249.5 25.3 %collective-permute-start.25 = (bf16[512,768]{1,0:T(8,128)(2,1)S(1)}, bf16[512,768]{1,0:T(8,128)(2,1)S(1)}, u32[]{:S(2)}, u32[]{:S(2)}) collective-permute-start(bf16[512,768]{1,0:T(8,128)(2,1)S(1)} %add_convert_fusion.5), channel_id=1, source_target_pairs={{0,8},{2,10},{4,12},{6,14},{8,0},{10,2},{12,4},{14,6},{17,25},{19,... | collective-permute-start | bytes 2359304 | tf_op jit(solution)/shard_map/ppermute | solution.py:103
  252.8 22.0 %collective-permute-start.27 = (bf16[512,768]{1,0:T(8,128)(2,1)S(1)}, bf16[512,768]{1,0:T(8,128)(2,1)S(1)}, u32[]{:S(2)}, u32[]{:S(2)}) collective-permute-start(bf16[512,768]{1,0:T(8,128)(2,1)S(1)} %add_convert_fusion.3), channel_id=1, source_target_pairs={{1,16},{3,18},{5,20},{7,22},{9,24},{11,26},{13,28},{15,30},{16,1},... | collective-permute-start | bytes 2359304 | tf_op jit(solution)/shard_map/ppermute | solution.py:103
  254.5 15.6 %copy-start.2 = (bf16[256,1024]{0,1:T(8,128)(2,1)S(1)}, bf16[256,1024]{0,1:T(8,128)(2,1)}, u32[]{:S(2)}) copy-start(bf16[256,1024]{0,1:T(8,128)(2,1)} %copy.11) | copy-start | bytes 1572868
  254.8 29.1 %collective-permute-start.30 = (bf16[512,768]{1,0:T(8,128)(2,1)S(1)}, bf16[512,768]{1,0:T(8,128)(2,1)S(1)}, u32[]{:S(2)}, u32[]{:S(2)}) collective-permute-start(bf16[512,768]{1,0:T(8,128)(2,1)S(1)} %add_convert_fusion.2), channel_id=1, source_target_pairs={{0,8},{2,10},{4,12},{6,14},{8,0},{10,2},{12,4},{14,6},{17,25},{19,... | collective-permute-start | bytes 2359304 | tf_op jit(solution)/shard_map/ppermute | solution.py:103
  259.7 24.1 %collective-permute-start.32 = (bf16[512,768]{1,0:T(8,128)(2,1)S(1)}, bf16[512,768]{1,0:T(8,128)(2,1)S(1)}, u32[]{:S(2)}, u32[]{:S(2)}) collective-permute-start(bf16[512,768]{1,0:T(8,128)(2,1)S(1)} %add_convert_fusion), channel_id=1, source_target_pairs={{1,16},{3,18},{5,20},{7,22},{9,24},{11,26},{13,28},{15,30},{16,1},... | collective-permute-start | bytes 2359304 | tf_op jit(solution)/shard_map/ppermute | solution.py:103
  287.5 18.6 %collective-permute-start.36 = (f32[256]{0:T(256)S(1)}, f32[256]{0:T(256)S(1)}, u32[]{:S(2)}, u32[]{:S(2)}) collective-permute-start(f32[256]{0:T(256)S(1)} %get-tuple-element.13), channel_id=1, source_target_pairs={{0,3},{1,0},{2,1},{3,2},{4,7},{5,4},{6,5},{7,6},{8,11},{9,8},{10,9... | collective-permute-start | bytes 3080 | tf_op jit(solution)/shard_map/ppermute | solution.py:103
  303.2 4.4 %collective-permute-start.37 = (f32[256]{0:T(256)S(1)}, f32[256]{0:T(256)S(1)}, u32[]{:S(2)}, u32[]{:S(2)}) collective-permute-start(f32[256]{0:T(256)S(1)} %get-tuple-element.12), channel_id=1, source_target_pairs={{0,2},{1,3},{2,0},{3,1},{4,6},{5,7},{6,4},{7,5},{8,10},{9,11},{10,... | collective-permute-start | bytes 3080 | tf_op jit(solution)/shard_map/ppermute | solution.py:103
  306.0 3.0 collective-permute-start.38
  309.2 3.7 %collective-permute-start.39 = (f32[4,8]{1,0:T(4,128)S(1)}, f32[4,8]{1,0:T(4,128)S(1)}, u32[]{:S(2)}, u32[]{:S(2)}) collective-permute-start(f32[4,8]{1,0:T(4,128)S(1)} %pad_maximum_fusion.6), channel_id=1, source_target_pairs={{0,4},{1,5},{2,6},{3,7},{4,0},{5,1},{6,2},{7,3},{8,12},{9,13},{10,... | collective-permute-start | bytes 392 | tf_op jit(solution)/shard_map/ppermute | solution.py:103
  312.8 5.4 %collective-permute-start.40 = (f32[4,8]{1,0:T(4,128)S(1)}, f32[4,8]{1,0:T(4,128)S(1)}, u32[]{:S(2)}, u32[]{:S(2)}) collective-permute-start(f32[4,8]{1,0:T(4,128)S(1)} %fusion.81), channel_id=1, source_target_pairs={{0,8},{1,9},{2,10},{3,11},{4,12},{5,13},{6,14},{7,15},{8,16},{9,17... | collective-permute-start | bytes 392 | tf_op jit(solution)/shard_map/ppermute | solution.py:103
  313.6 4.7 %collective-permute-start.41 = (f32[4,8]{1,0:T(4,128)S(1)}, f32[4,8]{1,0:T(4,128)S(1)}, u32[]{:S(2)}, u32[]{:S(2)}) collective-permute-start(f32[4,8]{1,0:T(4,128)S(1)} %fusion.81), channel_id=1, source_target_pairs={{0,16},{1,17},{2,18},{3,19},{4,20},{5,21},{6,22},{7,23},{8,24},{9,... | collective-permute-start | bytes 392 | tf_op jit(solution)/shard_map/ppermute | solution.py:103
  316.0 3.6 %collective-permute-start.42 = (f32[4,8]{1,0:T(4,128)S(1)}, f32[4,8]{1,0:T(4,128)S(1)}, u32[]{:S(2)}, u32[]{:S(2)}) collective-permute-start(f32[4,8]{1,0:T(4,128)S(1)} %fusion.81), channel_id=1, source_target_pairs={{0,24},{1,25},{2,26},{3,27},{4,28},{5,29},{6,30},{7,31},{8,0},{9,1... | collective-permute-start | bytes 392 | tf_op jit(solution)/shard_map/ppermute | solution.py:103

commit v3 on v2

--- a/solution.py
+++ b/solution.py
@@ -72,7 +72,7 @@
             pltpu.SemaphoreType.DMA((count,)),
             pltpu.SemaphoreType.DMA((count,)),
         ],
-        name="assemble",
+        name="as",
     )(where_to, local, *pieces)
 
 
@@ -208,32 +208,38 @@
         one = to_away(rows_at(factors, place * portion, portion))
         away = lax.dynamic_update_slice_in_dim(jnp.zeros_like(factors), one, place * portion, 0)
         for k in range(1, n_x):
-            away = lax.dynamic_update_slice_in_dim(away, to_x(one, k), ((place - k) % n_x) * portion, 0)
+            other = to_x(one, k)
+            away = lax.dynamic_update_slice_in_dim(away, other, ((place - k) % n_x) * portion, 0)
         factors = jnp.where(at_home, factors, away)
         factors = [factors[k * nf : (k + 1) * nf] for k in range(n_tile)]
         both = jnp.concatenate([activations, gradients], axis=1)
         both = [both] + [to_arch(both, k) for k in range(1, n_arch)]
         both = jnp.concatenate(both, axis=0)
 
-        parts = [cols_at(rotated_in, tile * width, width)]
-        for k in range(1, n_tile):
-            one = cols_at(rotated_in, ((tile + k) % n_tile) * width, width)
-            parts.append(to_tile(one, k))
-        scaled = []
-        for one_basis, one_factor in zip(bases, factors):
-            rotated = 0.0
-            for k, one in enumerate(parts):
-                rotated += mm_tn(rows_at(one_basis, ((tile - k) % n_tile) * nf, nf), one)
-            scaled.append((rotated * one_factor.astype(f32)).astype(bf16))
         restored = jnp.zeros((nd, nf), bf16)
-        for k in range(n_tile):
-            back = 0.0
-            for one_basis, one in zip(bases, scaled):
-                back += mm_tt(one, rows_at(one_basis, ((tile + k) % n_tile) * nf, nf))
-            back = back.astype(bf16)
-            if k:
-                back = to_tile(back, k)
-            restored = lax.dynamic_update_slice_in_dim(restored, back, ((tile - k) % n_tile) * width, 0)
+        chunk = width // 2
+        for c in range(width // chunk):
+            parts = []
+            for k in range(n_tile):
+                one = cols_at(rotated_in, ((tile + k) % n_tile) * width + c * chunk, chunk)
+                parts.append(to_tile(one, k) if k else one)
+            scaled = []
+            for one_basis, one_factor in zip(bases, factors):
+                rotated = 0.0
+                for k, one in enumerate(parts):
+                    rotated += mm_tn(rows_at(one_basis, ((tile - k) % n_tile) * nf, nf), one)
+                one_factor = one_factor[:, c * chunk : (c + 1) * chunk]
+                scaled.append((rotated * one_factor.astype(f32)).astype(bf16))
+            for k in reversed(range(n_tile)):
+                back = 0.0
+                for one_basis, one in zip(bases, scaled):
+                    back += mm_tt(one, rows_at(one_basis, ((tile + k) % n_tile) * nf, nf))
+                back = back.astype(bf16)
+                if k:
+                    back = to_tile(back, k)
+                restored = lax.dynamic_update_slice_in_dim(
+                    restored, back, ((tile - k) % n_tile) * width + c * chunk, 0
+                )
 
         hd = nd // 2
 
@@ -242,16 +248,20 @@
 
         outs = []
         for e in range(2):
+            added = []
             for s in range(1, n_half + 1):
                 theirs = product(other_base + at(-s), e).astype(bf16)
                 theirs = core(theirs)
-                added = product(own_base + at(-s), e) + theirs.astype(f32)
-                if s > 1:
-                    added = lax.optimization_barrier(added)
-                    away_total = (added + onward(away_total, False).astype(f32)).astype(bf16)
-                    home_total = (added + onward(home_total, True).astype(f32)).astype(bf16)
-                else:
-                    away_total = home_total = added.astype(bf16)
+                one = product(own_base + at(-s), e) + theirs.astype(f32)
+                added.append(one.astype(bf16) if s == 1 else lax.optimization_barrier(one))
+            away_total = added[0]
+            for one in added[1:]:
+                away_total = (one + onward(away_total, False).astype(f32)).astype(bf16)
+            if e == 0:
+                tick = send(away_total[:16, :128], lambda g, t, a: None if home(g, a) else (g, t, a ^ 1))
+            home_total, _ = lax.optimization_barrier((added[0], tick))
+            for one in added[1:]:
+                home_total = (one + onward(home_total, True).astype(f32)).astype(bf16)
             outs.append(jnp.where(at_home, home_total, cross(away_total)))
         preconditioned = jnp.concatenate(outs, axis=0)
         all_acts, all_grads = both[:, :nd], both[:, nd:]

time: 322 us -> 321 us (level)
  starting transfers between devices: 143 us -> 131 us
  matrix products: 42.9 us -> 51.8 us
  local copies, waits for them, and re-layouts: 24.4 us -> 19.6 us
  waiting for transfers between devices: 83.6 us -> 87.7 us
    ppermute x43 -> x46, starting transfers between devices: 143 us -> 131 us  [send(): return lax.ppermute(x, ('grp', 'tile', 'arch'), pairs)]
    dot_general x17, matrix products: 30.7 us -> 42.6 us  [mm(): lax.dot_general(a, b, (((1,), (0,)), ((), ())), preferred_element_type=f32)]
    ppermute x43 -> x46, waiting for transfers between devices: 83.6 us -> 87.7 us  [send(): return lax.ppermute(x, ('grp', 'tile', 'arch'), pairs)]
  transfers between devices with their start and end apart: 43 -> 46, of which waited for: 15 -> 15; matrix products, arithmetic and copies ran while one was open for 24% -> 24% of each run, Pallas kernels for 2% -> 2%
where the time goes in v3:
time: 321 us; the launch traced here: 319 us
  starting transfers between devices  131 us (41%)
  waiting for transfers between devices  87.7 us (27%)
  matrix products  51.8 us (16%)
  other arithmetic  20.5 us (6%)
  local copies, waits for them, and re-layouts  19.6 us (6%)
  Pallas kernels  7.2 us (2%)
    ppermute x46, starting transfers between devices, send(): return lax.ppermute(x, ('grp', 'tile', 'arch'), pairs)  131 us
    ppermute x46, waiting for transfers between devices, send(): return lax.ppermute(x, ('grp', 'tile', 'arch'), pairs)  87.7 us
    dot_general x17, matrix products, mm(): lax.dot_general(a, b, (((1,), (0,)), ((), ())), preferred_element_type=f32)  42.6 us
    pallas_call x1, Pallas kernels, assemble(): pl.pallas_call(kernel, out_shape=jax.ShapeDtypeStruct(local.shape, local....  7.2 us
  transfers between devices with their start and end apart: 46, of which 15 were waited for; matrix products, arithmetic and copies ran while one was open for 24% of the time, Pallas kernels for 2%

profile of v3, /device:TPU:0, one launch (start us, length us, event | category | flops | bytes accessed | tf_op | source)
XLA Modules:
  0.0 319.0 jit_solution(15946888338617157359)
XLA Ops:
  0.7 3.6 %divide_convert_fusion = bf16[768,1024]{1,0:T(8,128)(2,1)} fusion(f32[768,1024]{1,0:T(8,128)} %param.12), kind=kLoop, calls=%fused_computation.2 | loop fusion | flops 2359296 | bytes 4718592 | tf_op jit(solution)/shard_map/convert_element_type | solution.py:200
  4.3 2.5 constant_dynamic-slice_fusion.2
  6.8 4.9 %collective-permute-start.17 = (bf16[768,512]{1,0:T(8,128)(2,1)}, bf16[768,512]{1,0:T(8,128)(2,1)}, u32[]{:S(2)}, u32[]{:S(2)}) collective-permute-start(bf16[768,512]{1,0:T(8,128)(2,1)} %get-tuple-element.10), channel_id=1, source_target_pairs={{0,4},{2,6},{4,0},{6,2},{8,12},{10,14},{12,8},{14,10},{17,21},{19,... | collective-permute-start | bytes 2359304 | tf_op jit(solution)/shard_map/ppermute | solution.py:103
  13.0 1.5 collective-permute-start.12
  14.5 3.1 constant_dynamic-slice_fusion.4
  17.6 4.0 %collective-permute-start = (bf16[512,1024]{1,0:T(8,128)(2,1)}, bf16[512,1024]{1,0:T(8,128)(2,1)}, u32[]{:S(2)}, u32[]{:S(2)}) collective-permute-start(bf16[512,1024]{1,0:T(8,128)(2,1)} %get-tuple-element.7), channel_id=1, source_target_pairs={{0,16},{2,18},{4,20},{6,22},{8,24},{10,26},{12,28},{14,30},{17,1},... | collective-permute-start | bytes 3145736 | tf_op jit(solution)/shard_map/ppermute | solution.py:103
  21.6 2.3 collective-permute-start.4
  23.9 1.6 collective-permute-start.8
  25.5 1.8 fusion.62
  27.3 3.2 %collective-permute-start.18 = (bf16[768,512]{1,0:T(8,128)(2,1)}, bf16[768,512]{1,0:T(8,128)(2,1)}, u32[]{:S(2)}, u32[]{:S(2)}) collective-permute-start(bf16[768,512]{1,0:T(8,128)(2,1)} %fusion.62), channel_id=1, source_target_pairs={{0,16},{2,18},{4,20},{6,22},{8,24},{10,26},{12,28},{14,30},{17,1},... | collective-permute-start | bytes 2359304 | tf_op jit(solution)/shard_map/ppermute | solution.py:103
  33.2 11.3 %collective-permute-done.refs_0_ = bf16[512,1024]{1,0:T(8,128)(2,1)} collective-permute-done((bf16[512,1024]{1,0:T(8,128)(2,1)}, bf16[512,1024]{1,0:T(8,128)(2,1)}, u32[]{:S(2)}, u32[]{:S(2)}) %collective-permute-start) | collective-permute-done | bytes 1048608 | tf_op jit(solution)/shard_map/ppermute | solution.py:103
  44.5 1.6 collective-permute-start.1
  46.2 9.6 %collective-permute-done.4.refs_4_ = bf16[512,1024]{1,0:T(8,128)(2,1)} collective-permute-done((bf16[512,1024]{1,0:T(8,128)(2,1)}, bf16[512,1024]{1,0:T(8,128)(2,1)}, u32[]{:S(2)}, u32[]{:S(2)}) %collective-permute-start.4) | collective-permute-done | bytes 1048608 | tf_op jit(solution)/shard_map/ppermute | solution.py:103
  55.8 1.7 collective-permute-start.5
  57.5 2.7 broadcast_select_fusion
  60.2 49.2 %collective-permute-start.14 = (bf16[384,1024]{1,0:T(8,128)(2,1)}, bf16[384,1024]{1,0:T(8,128)(2,1)}, u32[]{:S(2)}, u32[]{:S(2)}) collective-permute-start(bf16[384,1024]{1,0:T(8,128)(2,1)} %get-tuple-element.12), channel_id=1, source_target_pairs={{0,8},{1,9},{2,10},{3,11},{4,12},{5,13},{6,14},{7,15},{8,0},{9,1},... | collective-permute-start | bytes 2359304 | tf_op jit(solution)/shard_map/ppermute | solution.py:103
  109.4 1.6 collective-permute-start.19
  110.9 4.1 %collective-permute-start.10 = (bf16[384,1024]{1,0:T(8,128)(2,1)}, bf16[384,1024]{1,0:T(8,128)(2,1)}, u32[]{:S(2)}, u32[]{:S(2)}) collective-permute-start(bf16[384,1024]{1,0:T(8,128)(2,1)} %get-tuple-element.13), channel_id=1, source_target_pairs={{0,8},{1,9},{2,10},{3,11},{4,12},{5,13},{6,14},{7,15},{8,0},{9,1},... | collective-permute-start | bytes 2359304 | tf_op jit(solution)/shard_map/ppermute | solution.py:103
  115.0 14.2 %collective-permute-done.14 = bf16[384,1024]{1,0:T(8,128)(2,1)} collective-permute-done((bf16[384,1024]{1,0:T(8,128)(2,1)}, bf16[384,1024]{1,0:T(8,128)(2,1)}, u32[]{:S(2)}, u32[]{:S(2)}) %collective-permute-start.14) | collective-permute-done | bytes 786464 | tf_op jit(solution)/shard_map/ppermute | solution.py:103
  129.2 1.6 collective-permute-start.2
  130.8 1.6 collective-permute-start.6
  132.5 1.7 collective-permute-start.3
  134.1 1.7 collective-permute-start.7
  135.8 2.0 copy.11
  141.4 1.8 constant_dynamic-update-slice_fusion.5
  144.4 1.6 collective-permute-done.10
  146.0 4.2 %collective-permute-start.13 = (bf16[384,1024]{1,0:T(8,128)(2,1)}, bf16[384,1024]{1,0:T(8,128)(2,1)}, u32[]{:S(2)}, u32[]{:S(2)}) collective-permute-start(bf16[384,1024]{1,0:T(8,128)(2,1)} %get-tuple-element.12), channel_id=1, source_target_pairs={{0,1},{1,0},{2,3},{3,2},{4,5},{5,4},{6,7},{7,6},{8,9},{9,8},{10,11... | collective-permute-start | bytes 2359304 | tf_op jit(solution)/shard_map/ppermute | solution.py:103
  150.3 2.7 fusion.18
  153.5 4.1 %collective-permute-start.15 = (bf16[384,1024]{1,0:T(8,128)(2,1)}, bf16[384,1024]{1,0:T(8,128)(2,1)}, u32[]{:S(2)}, u32[]{:S(2)}) collective-permute-start(bf16[384,1024]{1,0:T(8,128)(2,1)} %collective-permute-done.14), channel_id=1, source_target_pairs={{0,1},{1,0},{2,3},{3,2},{4,5},{5,4},{6,7},{7,6},{8,9},{9,8},{10,11... | collective-permute-start | bytes 2359304 | tf_op jit(solution)/shard_map/ppermute | solution.py:103
  157.7 2.6 collective-permute-start.11
  160.3 7.2 %as.1 = bf16[4096,1024]{1,0:T(8,128)(2,1)} custom-call(s32[9]{0:T(128)} %stack.43.where_ref, bf16[4096,1024]{1,0:T(8,128)(2,1)} %local_ref.1, bf16[512,1024]{1,0:T(8,128)(2,1)} %collective-permute-done.refs_0_, bf16[512,1024]{1,0:T(8,128)(2,1)} %collective-permute-done.1.refs_1_, bf16[512,1024]{1,0:T(8,128)(2,1)} %collective-permute-done.2.refs_2_, ...), custom_call_target="tpu_custom_call" | custom-call | tf_op jit(solution)/shard_map/as/pallas_call | solution.py:65
  167.5 3.0 fusion.6
  170.4 3.1 fusion.8
  173.5 2.1 fusion.10
  176.7 2.1 fusion.2
  178.9 2.1 fusion.4
  181.0 2.2 add_convert_fusion.6
  183.2 2.2 add_convert_fusion.7
  191.0 6.6 %collective-permute-done.23 = bf16[768,256]{1,0:T(8,128)(2,1)S(1)} collective-permute-done((bf16[768,256]{1,0:T(8,128)(2,1)S(1)}, bf16[768,256]{1,0:T(8,128)(2,1)S(1)}, u32[]{:S(2)}, u32[]{:S(2)}) %collective-permute-start.23) | collective-permute-done | bytes 393248 | tf_op jit(solution)/shard_map/ppermute | solution.py:103
  201.8 4.2 %collective-permute-done.16 = bf16[768,256]{1,0:T(8,128)(2,1)S(1)} collective-permute-done((bf16[768,256]{1,0:T(8,128)(2,1)S(1)}, bf16[768,256]{1,0:T(8,128)(2,1)S(1)}, u32[]{:S(2)}, u32[]{:S(2)}) %collective-permute-start.16) | collective-permute-done | bytes 393248 | tf_op jit(solution)/shard_map/ppermute | solution.py:103
  211.5 10.4 %collective-permute-done.22 = bf16[256,768]{1,0:T(8,128)(2,1)S(1)} collective-permute-done((bf16[256,768]{1,0:T(8,128)(2,1)S(1)}, bf16[256,768]{1,0:T(8,128)(2,1)S(1)}, u32[]{:S(2)}, u32[]{:S(2)}) %collective-permute-start.22) | collective-permute-done | bytes 393248 | tf_op jit(solution)/shard_map/ppermute | solution.py:103
  223.2 1.9 convolution_convert_fusion.2
  227.9 2.8 convolution_convert_fusion.3
  231.1 2.2 convolution_convert_fusion
  233.6 2.4 add_convert_fusion.5
  236.8 3.1 convolution_convert_fusion.1
  239.9 1.5 collective-permute-start.31
  241.4 2.2 convert_add_fusion.1
  243.7 3.7 %add_convert_fusion.2 = bf16[512,768]{1,0:T(8,128)(2,1)} fusion(bf16[512,768]{1,0:T(8,128)(2,1)S(1)} %collective-permute-done.32, bf16[1024,768]{1,0:T(8,128)(2,1)S(1)} %copy-done.10, bf16[4096,1024]{1,0:T(8,128)(2,1)} %as.1, s32[]{:T(128)S(6)} %select_n.369), kind=kOutput, calls=%fused_computation.36 | convolution fusion | flops 806486016 | bytes 4194308 | tf_op jit(solution)/shard_map/dot_general | solution.py:14
  247.3 1.5 collective-permute-start.34
  251.3 2.5 collective-permute-done.28
  255.3 3.2 collective-permute-start.29
  258.5 2.9 convert_add_fusion
  263.6 2.9 collective-permute-start.33
  267.3 4.9 %pad_maximum_fusion = bf16[1024,1792]{0,1:T(8,128)(2,1)S(1)} fusion(bf16[256,1792]{0,1:T(8,128)(2,1)} %collective-permute-done.38, bf16[256,1792]{0,1:T(8,128)(2,1)} %collective-permute-done.37, bf16[256,1792]{0,1:T(8,128)(2,1)} %collective-permute-done.36, bf16[256,768]{0,1:T(8,128)(2,1)S(1)} %copy.12, bf16[256,1024]{0,1:T(8,128)(2,1)S(1)} %copy-done.7), kind=kLoop, calls=%fused_computation | loop fusion | flops 18350080 | bytes 7340032 | tf_op jit(solution)/shard_map/concatenate | solution.py:217
  272.3 5.6 %collective-permute-done.29 = bf16[512,768]{1,0:T(8,128)(2,1)S(1)} collective-permute-done((bf16[512,768]{1,0:T(8,128)(2,1)}, bf16[512,768]{1,0:T(8,128)(2,1)S(1)}, u32[]{:S(2)}, u32[]{:S(2)}) %collective-permute-start.29) | collective-permute-done | bytes 786464 | tf_op jit(solution)/shard_map/ppermute | solution.py:103
  278.1 15.2 %collective-permute-done.33 = bf16[512,768]{1,0:T(8,128)(2,1)S(1)} collective-permute-done((bf16[512,768]{1,0:T(8,128)(2,1)}, bf16[512,768]{1,0:T(8,128)(2,1)S(1)}, u32[]{:S(2)}, u32[]{:S(2)}) %collective-permute-start.33) | collective-permute-done | bytes 786464 | tf_op jit(solution)/shard_map/ppermute | solution.py:103
  293.6 3.5 %multiply_reduce_fusion = f32[1024]{0:T(1024)S(1)} fusion(bf16[256,1792]{0,1:T(8,128)(2,1)} %collective-permute-done.38, bf16[256,1792]{0,1:T(8,128)(2,1)} %collective-permute-done.37, bf16[256,1792]{0,1:T(8,128)(2,1)} %collective-permute-done.36, bf16[256,768]{0,1:T(8,128)(2,1)S(1)} %copy.12, bf16[256,1024]{0,1:T(8,128)(2,1)S(1)} %copy-done.7, ...), kind=kOutput, calls=%fused_computation.1 | convolution fusion | flops 1623194624 | bytes 7344128 | tf_op jit(solution)/shard_map/dot_general | solution.py:14
  297.1 3.1 collective-permute-start.39
  301.6 2.2 collective-permute-done.40
  304.5 1.5 collective-permute-start.42
  308.2 5.8 %collective-permute-start.43 = (f32[4,8]{1,0:T(4,128)S(1)}, f32[4,8]{1,0:T(4,128)S(1)}, u32[]{:S(2)}, u32[]{:S(2)}) collective-permute-start(f32[4,8]{1,0:T(4,128)S(1)} %fusion.113), channel_id=1, source_target_pairs={{0,8},{1,9},{2,10},{3,11},{4,12},{5,13},{6,14},{7,15},{8,16},{9,17... | collective-permute-start | bytes 392 | tf_op jit(solution)/shard_map/ppermute | solution.py:103
  313.9 2.4 collective-permute-start.45
  316.4 2.0 collective-permute-done.44
  (133 shorter events, 43.0 us)
Async XLA Ops:
  0.6 29.9 %copy-start = (bf16[1536,768]{1,0:T(8,128)(2,1)S(1)}, bf16[1536,768]{1,0:T(8,128)(2,1)}, u32[]{:S(2)}) copy-start(bf16[1536,768]{1,0:T(8,128)(2,1)} %param.11) | copy-start | bytes 7077892
  4.3 7.4 %copy-start.4 = (bf16[1,768,1024]{2,1,0:T(8,128)(2,1)S(1)}, bf16[1,768,1024]{2,1,0:T(8,128)(2,1)}, u32[]{:S(2)}) copy-start(bf16[1,768,1024]{2,1,0:T(8,128)(2,1)} %param.9) | copy-start | bytes 4718596
  6.8 18.7 %collective-permute-start.17 = (bf16[768,512]{1,0:T(8,128)(2,1)}, bf16[768,512]{1,0:T(8,128)(2,1)}, u32[]{:S(2)}, u32[]{:S(2)}) collective-permute-start(bf16[768,512]{1,0:T(8,128)(2,1)} %get-tuple-element.10), channel_id=1, source_target_pairs={{0,4},{2,6},{4,0},{6,2},{8,12},{10,14},{12,8},{14,10},{17,21},{19,... | collective-permute-start | bytes 2359304 | tf_op jit(solution)/shard_map/ppermute | solution.py:103
  13.0 18.6 %collective-permute-start.12 = (bf16[384,1024]{1,0:T(8,128)(2,1)}, bf16[384,1024]{1,0:T(8,128)(2,1)}, u32[]{:S(2)}, u32[]{:S(2)}) collective-permute-start(bf16[384,1024]{1,0:T(8,128)(2,1)} %get-tuple-element.14), channel_id=1, source_target_pairs={{1,16},{3,18},{5,20},{7,22},{9,24},{11,26},{13,28},{15,30},{16,1},... | collective-permute-start | bytes 2359304 | tf_op jit(solution)/shard_map/ppermute | solution.py:103
  17.6 26.9 %collective-permute-start = (bf16[512,1024]{1,0:T(8,128)(2,1)}, bf16[512,1024]{1,0:T(8,128)(2,1)}, u32[]{:S(2)}, u32[]{:S(2)}) collective-permute-start(bf16[512,1024]{1,0:T(8,128)(2,1)} %get-tuple-element.7), channel_id=1, source_target_pairs={{0,16},{2,18},{4,20},{6,22},{8,24},{10,26},{12,28},{14,30},{17,1},... | collective-permute-start | bytes 3145736 | tf_op jit(solution)/shard_map/ppermute | solution.py:103
  21.6 34.2 %collective-permute-start.4 = (bf16[512,1024]{1,0:T(8,128)(2,1)}, bf16[512,1024]{1,0:T(8,128)(2,1)}, u32[]{:S(2)}, u32[]{:S(2)}) collective-permute-start(bf16[512,1024]{1,0:T(8,128)(2,1)} %get-tuple-element.6), channel_id=1, source_target_pairs={{0,16},{2,18},{4,20},{6,22},{8,24},{10,26},{12,28},{14,30},{17,1},... | collective-permute-start | bytes 3145736 | tf_op jit(solution)/shard_map/ppermute | solution.py:103
  23.9 33.5 %collective-permute-start.8 = (bf16[384,1024]{1,0:T(8,128)(2,1)}, bf16[384,1024]{1,0:T(8,128)(2,1)}, u32[]{:S(2)}, u32[]{:S(2)}) collective-permute-start(bf16[384,1024]{1,0:T(8,128)(2,1)} %get-tuple-element.15), channel_id=1, source_target_pairs={{1,16},{3,18},{5,20},{7,22},{9,24},{11,26},{13,28},{15,30},{16,1},... | collective-permute-start | bytes 2359304 | tf_op jit(solution)/shard_map/ppermute | solution.py:103
  27.3 82.0 %collective-permute-start.18 = (bf16[768,512]{1,0:T(8,128)(2,1)}, bf16[768,512]{1,0:T(8,128)(2,1)}, u32[]{:S(2)}, u32[]{:S(2)}) collective-permute-start(bf16[768,512]{1,0:T(8,128)(2,1)} %fusion.62), channel_id=1, source_target_pairs={{0,16},{2,18},{4,20},{6,22},{8,24},{10,26},{12,28},{14,30},{17,1},... | collective-permute-start | bytes 2359304 | tf_op jit(solution)/shard_map/ppermute | solution.py:103
  31.6 79.3 %collective-permute-start.20 = (bf16[768,768]{1,0:T(8,128)(2,1)}, bf16[768,768]{1,0:T(8,128)(2,1)}, u32[]{:S(2)}, u32[]{:S(2)}) collective-permute-start(bf16[768,768]{1,0:T(8,128)(2,1)} %constant_dynamic-slice_fusion.1), channel_id=1, source_target_pairs={{0,4},{1,5},{2,6},{3,7},{4,0},{5,1},{6,2},{7,3},{8,12},{9,13},{10,... | collective-permute-start | bytes 3538952 | tf_op jit(solution)/shard_map/ppermute | solution.py:103
  44.5 86.3 %collective-permute-start.1 = (bf16[512,1024]{1,0:T(8,128)(2,1)}, bf16[512,1024]{1,0:T(8,128)(2,1)}, u32[]{:S(2)}, u32[]{:S(2)}) collective-permute-start(bf16[512,1024]{1,0:T(8,128)(2,1)} %collective-permute-done.refs_0_), channel_id=1, source_target_pairs={{1,5},{3,7},{5,1},{7,3},{9,13},{11,15},{13,9},{15,11},{16,20},{18,... | collective-permute-start | bytes 3145736 | tf_op jit(solution)/shard_map/ppermute | solution.py:103
  55.8 76.7 %collective-permute-start.5 = (bf16[512,1024]{1,0:T(8,128)(2,1)}, bf16[512,1024]{1,0:T(8,128)(2,1)}, u32[]{:S(2)}, u32[]{:S(2)}) collective-permute-start(bf16[512,1024]{1,0:T(8,128)(2,1)} %collective-permute-done.4.refs_4_), channel_id=1, source_target_pairs={{1,3},{3,1},{5,7},{7,5},{9,11},{11,9},{13,15},{15,13},{16,18},{18,... | collective-permute-start | bytes 3145736 | tf_op jit(solution)/shard_map/ppermute | solution.py:103
  60.2 69.0 %collective-permute-start.14 = (bf16[384,1024]{1,0:T(8,128)(2,1)}, bf16[384,1024]{1,0:T(8,128)(2,1)}, u32[]{:S(2)}, u32[]{:S(2)}) collective-permute-start(bf16[384,1024]{1,0:T(8,128)(2,1)} %get-tuple-element.12), channel_id=1, source_target_pairs={{0,8},{1,9},{2,10},{3,11},{4,12},{5,13},{6,14},{7,15},{8,0},{9,1},... | collective-permute-start | bytes 2359304 | tf_op jit(solution)/shard_map/ppermute | solution.py:103
  109.4 24.8 %collective-permute-start.19 = (bf16[768,512]{1,0:T(8,128)(2,1)}, bf16[768,512]{1,0:T(8,128)(2,1)}, u32[]{:S(2)}, u32[]{:S(2)}) collective-permute-start(bf16[768,512]{1,0:T(8,128)(2,1)} %collective-permute-done.18), channel_id=1, source_target_pairs={{1,3},{3,1},{5,7},{7,5},{9,11},{11,9},{13,15},{15,13},{16,18},{18,... | collective-permute-start | bytes 2359304 | tf_op jit(solution)/shard_map/ppermute | solution.py:103
  110.9 35.1 %collective-permute-start.10 = (bf16[384,1024]{1,0:T(8,128)(2,1)}, bf16[384,1024]{1,0:T(8,128)(2,1)}, u32[]{:S(2)}, u32[]{:S(2)}) collective-permute-start(bf16[384,1024]{1,0:T(8,128)(2,1)} %get-tuple-element.13), channel_id=1, source_target_pairs={{0,8},{1,9},{2,10},{3,11},{4,12},{5,13},{6,14},{7,15},{8,0},{9,1},... | collective-permute-start | bytes 2359304 | tf_op jit(solution)/shard_map/ppermute | solution.py:103
  129.2 23.8 %collective-permute-start.2 = (bf16[512,1024]{1,0:T(8,128)(2,1)}, bf16[512,1024]{1,0:T(8,128)(2,1)}, u32[]{:S(2)}, u32[]{:S(2)}) collective-permute-start(bf16[512,1024]{1,0:T(8,128)(2,1)} %collective-permute-done.refs_0_), channel_id=1, source_target_pairs={{1,3},{3,1},{5,7},{7,5},{9,11},{11,9},{13,15},{15,13},{16,18},{18,... | collective-permute-start | bytes 3145736 | tf_op jit(solution)/shard_map/ppermute | solution.py:103
  130.8 22.2 %collective-permute-start.6 = (bf16[512,1024]{1,0:T(8,128)(2,1)}, bf16[512,1024]{1,0:T(8,128)(2,1)}, u32[]{:S(2)}, u32[]{:S(2)}) collective-permute-start(bf16[512,1024]{1,0:T(8,128)(2,1)} %collective-permute-done.4.refs_4_), channel_id=1, source_target_pairs={{1,5},{3,7},{5,1},{7,3},{9,13},{11,15},{13,9},{15,11},{16,20},{18,... | collective-permute-start | bytes 3145736 | tf_op jit(solution)/shard_map/ppermute | solution.py:103
  132.5 21.1 %collective-permute-start.3 = (bf16[512,1024]{1,0:T(8,128)(2,1)}, bf16[512,1024]{1,0:T(8,128)(2,1)}, u32[]{:S(2)}, u32[]{:S(2)}) collective-permute-start(bf16[512,1024]{1,0:T(8,128)(2,1)} %collective-permute-done.1.refs_1_), channel_id=1, source_target_pairs={{1,3},{3,1},{5,7},{7,5},{9,11},{11,9},{13,15},{15,13},{16,18},{18,... | collective-permute-start | bytes 3145736 | tf_op jit(solution)/shard_map/ppermute | solution.py:103
  134.1 23.5 %collective-permute-start.7 = (bf16[512,1024]{1,0:T(8,128)(2,1)}, bf16[512,1024]{1,0:T(8,128)(2,1)}, u32[]{:S(2)}, u32[]{:S(2)}) collective-permute-start(bf16[512,1024]{1,0:T(8,128)(2,1)} %collective-permute-done.5.refs_5_), channel_id=1, source_target_pairs={{1,5},{3,7},{5,1},{7,3},{9,13},{11,15},{13,9},{15,11},{16,20},{18,... | collective-permute-start | bytes 3145736 | tf_op jit(solution)/shard_map/ppermute | solution.py:103
  141.3 1.9 copy-start.1
  146.0 27.5 %collective-permute-start.13 = (bf16[384,1024]{1,0:T(8,128)(2,1)}, bf16[384,1024]{1,0:T(8,128)(2,1)}, u32[]{:S(2)}, u32[]{:S(2)}) collective-permute-start(bf16[384,1024]{1,0:T(8,128)(2,1)} %get-tuple-element.12), channel_id=1, source_target_pairs={{0,1},{1,0},{2,3},{3,2},{4,5},{5,4},{6,7},{7,6},{8,9},{9,8},{10,11... | collective-permute-start | bytes 2359304 | tf_op jit(solution)/shard_map/ppermute | solution.py:103
  153.0 22.7 %collective-permute-start.9 = (bf16[384,1024]{1,0:T(8,128)(2,1)}, bf16[384,1024]{1,0:T(8,128)(2,1)S(1)}, u32[]{:S(2)}, u32[]{:S(2)}) collective-permute-start(bf16[384,1024]{1,0:T(8,128)(2,1)} %get-tuple-element.13), channel_id=1, source_target_pairs={{0,1},{1,0},{2,3},{3,2},{4,5},{5,4},{6,7},{7,6},{8,9},{9,8},{10,11... | collective-permute-start | bytes 2359304 | tf_op jit(solution)/shard_map/ppermute | solution.py:103
  153.0 34.0 %collective-permute-start.21 = (bf16[768,768]{1,0:T(8,128)(2,1)}, bf16[768,768]{1,0:T(8,128)(2,1)}, u32[]{:S(2)}, u32[]{:S(2)}) collective-permute-start(bf16[768,768]{1,0:T(8,128)(2,1)} %collective-permute-done.20), channel_id=1, source_target_pairs={{0,1},{1,0},{2,3},{3,2},{4,5},{5,4},{6,7},{7,6},{8,9},{9,8},{10,11... | collective-permute-start | bytes 3538952 | tf_op jit(solution)/shard_map/ppermute | solution.py:103
  153.5 23.2 %collective-permute-start.15 = (bf16[384,1024]{1,0:T(8,128)(2,1)}, bf16[384,1024]{1,0:T(8,128)(2,1)}, u32[]{:S(2)}, u32[]{:S(2)}) collective-permute-start(bf16[384,1024]{1,0:T(8,128)(2,1)} %collective-permute-done.14), channel_id=1, source_target_pairs={{0,1},{1,0},{2,3},{3,2},{4,5},{5,4},{6,7},{7,6},{8,9},{9,8},{10,11... | collective-permute-start | bytes 2359304 | tf_op jit(solution)/shard_map/ppermute | solution.py:103
  157.7 21.2 %collective-permute-start.11 = (bf16[384,1024]{1,0:T(8,128)(2,1)}, bf16[384,1024]{1,0:T(8,128)(2,1)}, u32[]{:S(2)}, u32[]{:S(2)}) collective-permute-start(bf16[384,1024]{1,0:T(8,128)(2,1)} %collective-permute-done.10), channel_id=1, source_target_pairs={{0,1},{1,0},{2,3},{3,2},{4,5},{5,4},{6,7},{7,6},{8,9},{9,8},{10,11... | collective-permute-start | bytes 2359304 | tf_op jit(solution)/shard_map/ppermute | solution.py:103
  167.5 6.1 %copy-start.3 = (bf16[4096,1024]{1,0:T(8,128)(2,1)S(1)}, bf16[4096,1024]{1,0:T(8,128)(2,1)}, u32[]{:S(2)}) copy-start(bf16[4096,1024]{1,0:T(8,128)(2,1)} %as.1) | copy-start | bytes 25165828
  185.4 1.7 copy-start.2
  185.5 12.1 %collective-permute-start.23 = (bf16[768,256]{1,0:T(8,128)(2,1)S(1)}, bf16[768,256]{1,0:T(8,128)(2,1)S(1)}, u32[]{:S(2)}, u32[]{:S(2)}) collective-permute-start(bf16[768,256]{1,0:T(8,128)(2,1)S(1)} %get-tuple-element.8), channel_id=1, source_target_pairs={{0,4},{1,5},{2,6},{3,7},{4,0},{5,1},{6,2},{7,3},{8,12},{9,13},{10,... | collective-permute-start | bytes 1179656 | tf_op jit(solution)/shard_map/ppermute | solution.py:103
  188.4 17.6 %collective-permute-start.16 = (bf16[768,256]{1,0:T(8,128)(2,1)S(1)}, bf16[768,256]{1,0:T(8,128)(2,1)S(1)}, u32[]{:S(2)}, u32[]{:S(2)}) collective-permute-start(bf16[768,256]{1,0:T(8,128)(2,1)S(1)} %get-tuple-element.9), channel_id=1, source_target_pairs={{0,4},{1,5},{2,6},{3,7},{4,0},{5,1},{6,2},{7,3},{8,12},{9,13},{10,... | collective-permute-start | bytes 1179656 | tf_op jit(solution)/shard_map/ppermute | solution.py:103
  191.0 7.1 %copy-start.8 = (bf16[1536,512]{1,0:T(8,128)(2,1)S(1)}, bf16[1536,512]{1,0:T(8,128)(2,1)}, u32[]{:S(2)}) copy-start(bf16[1536,512]{1,0:T(8,128)(2,1)} %fusion.18) | copy-start | bytes 4718596
  200.3 22.3 %collective-permute-start.24 = (bf16[256,768]{1,0:T(8,128)(2,1)S(1)}, bf16[256,768]{1,0:T(8,128)(2,1)S(1)}, u32[]{:S(2)}, u32[]{:S(2)}) collective-permute-start(bf16[256,768]{1,0:T(8,128)(2,1)S(1)} %fusion.36), channel_id=1, source_target_pairs={{0,4},{1,5},{2,6},{3,7},{4,0},{5,1},{6,2},{7,3},{8,12},{9,13},{10,... | collective-permute-start | bytes 1179656 | tf_op jit(solution)/shard_map/ppermute | solution.py:103
  208.9 13.0 %collective-permute-start.22 = (bf16[256,768]{1,0:T(8,128)(2,1)S(1)}, bf16[256,768]{1,0:T(8,128)(2,1)S(1)}, u32[]{:S(2)}, u32[]{:S(2)}) collective-permute-start(bf16[256,768]{1,0:T(8,128)(2,1)S(1)} %fusion.31), channel_id=1, source_target_pairs={{0,4},{1,5},{2,6},{3,7},{4,0},{5,1},{6,2},{7,3},{8,12},{9,13},{10,... | collective-permute-start | bytes 1179656 | tf_op jit(solution)/shard_map/ppermute | solution.py:103
  223.2 1.9 copy-start.9
  223.2 1.9 copy-start.7
  225.1 2.6 copy-start.13
  225.1 8.5 %collective-permute-start.26 = (bf16[512,768]{1,0:T(8,128)(2,1)}, bf16[512,768]{1,0:T(8,128)(2,1)}, u32[]{:S(2)}, u32[]{:S(2)}) collective-permute-start(bf16[512,768]{1,0:T(8,128)(2,1)} %convolution_convert_fusion.2), channel_id=1, source_target_pairs={{0,1},{1,0},{2,3},{3,2},{4,5},{5,4},{6,7},{7,6},{8,9},{9,8},{10,11... | collective-permute-start | bytes 2359304 | tf_op jit(solution)/shard_map/ppermute | solution.py:103
  226.2 36.6 %collective-permute-start.36 = (bf16[256,1792]{0,1:T(8,128)(2,1)}, bf16[256,1792]{0,1:T(8,128)(2,1)}, u32[]{:S(2)}, u32[]{:S(2)}) collective-permute-start(bf16[256,1792]{0,1:T(8,128)(2,1)} %pad_maximum_fusion.4), channel_id=1, source_target_pairs={{0,1},{1,2},{2,3},{3,0},{4,5},{5,6},{6,7},{7,4},{8,9},{9,10},{10,1... | collective-permute-start | bytes 2752520 | tf_op jit(solution)/shard_map/ppermute | solution.py:103
  226.7 36.9 %collective-permute-start.37 = (bf16[256,1792]{0,1:T(8,128)(2,1)}, bf16[256,1792]{0,1:T(8,128)(2,1)}, u32[]{:S(2)}, u32[]{:S(2)}) collective-permute-start(bf16[256,1792]{0,1:T(8,128)(2,1)} %pad_maximum_fusion.4), channel_id=1, source_target_pairs={{0,2},{1,3},{2,0},{3,1},{4,6},{5,7},{6,4},{7,5},{8,10},{9,11},{10,... | collective-permute-start | bytes 2752520 | tf_op jit(solution)/shard_map/ppermute | solution.py:103
  227.9 3.2 %copy-start.10 = (bf16[1024,768]{1,0:T(8,128)(2,1)S(1)}, bf16[1024,768]{1,0:T(8,128)(2,1)}, u32[]{:S(2)}) copy-start(bf16[1024,768]{1,0:T(8,128)(2,1)} %copy-done.9) | copy-start | bytes 4718596
  230.7 9.2 %collective-permute-start.25 = (bf16[512,768]{1,0:T(8,128)(2,1)S(1)}, bf16[512,768]{1,0:T(8,128)(2,1)S(1)}, u32[]{:S(2)}, u32[]{:S(2)}) collective-permute-start(bf16[512,768]{1,0:T(8,128)(2,1)S(1)} %convolution_convert_fusion.3), channel_id=1, source_target_pairs={{0,1},{1,0},{2,3},{3,2},{4,5},{5,4},{6,7},{7,6},{8,9},{9,8},{10,11... | collective-permute-start | bytes 2359304 | tf_op jit(solution)/shard_map/ppermute | solution.py:103
  233.3 10.3 %collective-permute-start.32 = (bf16[512,768]{1,0:T(8,128)(2,1)S(1)}, bf16[512,768]{1,0:T(8,128)(2,1)S(1)}, u32[]{:S(2)}, u32[]{:S(2)}) collective-permute-start(bf16[512,768]{1,0:T(8,128)(2,1)S(1)} %convolution_convert_fusion), channel_id=1, source_target_pairs={{0,1},{1,0},{2,3},{3,2},{4,5},{5,4},{6,7},{7,6},{8,9},{9,8},{10,11... | collective-permute-start | bytes 2359304 | tf_op jit(solution)/shard_map/ppermute | solution.py:103
  236.0 3.8 %copy-start.12 = (bf16[512,768]{1,0:T(8,128)(2,1)}, bf16[512,768]{1,0:T(8,128)(2,1)S(1)}, u32[]{:S(2)}) copy-start(bf16[512,768]{1,0:T(8,128)(2,1)S(1)} %add_convert_fusion.5) | copy-start | bytes 2359300
  236.0 12.8 %collective-permute-start.27 = (bf16[512,768]{1,0:T(8,128)(2,1)S(1)}, bf16[512,768]{1,0:T(8,128)(2,1)S(1)}, u32[]{:S(2)}, u32[]{:S(2)}) collective-permute-start(bf16[512,768]{1,0:T(8,128)(2,1)S(1)} %add_convert_fusion.5), channel_id=1, source_target_pairs={{1,9},{3,11},{5,13},{7,15},{9,1},{11,3},{13,5},{15,7},{16,24},{18,... | collective-permute-start | bytes 2359304 | tf_op jit(solution)/shard_map/ppermute | solution.py:103
  239.9 14.8 %collective-permute-start.31 = (bf16[512,768]{1,0:T(8,128)(2,1)}, bf16[512,768]{1,0:T(8,128)(2,1)}, u32[]{:S(2)}, u32[]{:S(2)}) collective-permute-start(bf16[512,768]{1,0:T(8,128)(2,1)} %convolution_convert_fusion.1), channel_id=1, source_target_pairs={{0,1},{1,0},{2,3},{3,2},{4,5},{5,4},{6,7},{7,6},{8,9},{9,8},{10,11... | collective-permute-start | bytes 2359304 | tf_op jit(solution)/shard_map/ppermute | solution.py:103
  243.6 5.3 %copy-start.5 = (f32[512,768]{1,0:T(8,128)}, f32[512,768]{1,0:T(8,128)S(1)}, u32[]{:S(2)}) copy-start(f32[512,768]{1,0:T(8,128)S(1)} %convert_add_fusion.1) | copy-start | bytes 4718596
  247.3 8.0 %collective-permute-start.34 = (bf16[512,768]{1,0:T(8,128)(2,1)}, bf16[512,768]{1,0:T(8,128)(2,1)}, u32[]{:S(2)}, u32[]{:S(2)}) collective-permute-start(bf16[512,768]{1,0:T(8,128)(2,1)} %add_convert_fusion.2), channel_id=1, source_target_pairs={{1,9},{3,11},{5,13},{7,15},{9,1},{11,3},{13,5},{15,7},{16,24},{18,... | collective-permute-start | bytes 2359304 | tf_op jit(solution)/shard_map/ppermute | solution.py:103
  249.1 0.9 copy-start.11
  250.0 3.8 %collective-permute-start.28 = (bf16[16,128]{1,0:T(8,128)(2,1)S(1)}, bf16[16,128]{1,0:T(8,128)(2,1)S(1)}, u32[]{:S(2)}, u32[]{:S(2)}) collective-permute-start(bf16[16,128]{1,0:T(8,128)(2,1)S(1)} %slice.74), channel_id=1, source_target_pairs={{1,0},{3,2},{5,4},{7,6},{9,8},{11,10},{13,12},{15,14},{16,17},{18,... | collective-permute-start | bytes 12296 | tf_op jit(solution)/shard_map/ppermute | solution.py:103
  253.7 13.6 %collective-permute-start.38 = (bf16[256,1792]{0,1:T(8,128)(2,1)}, bf16[256,1792]{0,1:T(8,128)(2,1)}, u32[]{:S(2)}, u32[]{:S(2)}) collective-permute-start(bf16[256,1792]{0,1:T(8,128)(2,1)} %pad_maximum_fusion.4), channel_id=1, source_target_pairs={{0,3},{1,0},{2,1},{3,2},{4,7},{5,4},{6,5},{7,6},{8,11},{9,8},{10,9... | collective-permute-start | bytes 2752520 | tf_op jit(solution)/shard_map/ppermute | solution.py:103
  254.6 17.7 %collective-permute-start.30 = (bf16[512,768]{1,0:T(8,128)(2,1)}, bf16[512,768]{1,0:T(8,128)(2,1)S(1)}, u32[]{:S(2)}, u32[]{:S(2)}) collective-permute-start(bf16[512,768]{1,0:T(8,128)(2,1)} %copy-done.11), channel_id=1, source_target_pairs={{1,16},{3,18},{5,20},{7,22},{9,24},{11,26},{13,28},{15,30},{16,1},... | collective-permute-start | bytes 2359304 | tf_op jit(solution)/shard_map/ppermute | solution.py:103
  255.3 22.5 %collective-permute-start.29 = (bf16[512,768]{1,0:T(8,128)(2,1)}, bf16[512,768]{1,0:T(8,128)(2,1)S(1)}, u32[]{:S(2)}, u32[]{:S(2)}) collective-permute-start(bf16[512,768]{1,0:T(8,128)(2,1)} %copy-done.12), channel_id=1, source_target_pairs={{0,8},{2,10},{4,12},{6,14},{8,0},{10,2},{12,4},{14,6},{17,25},{19,... | collective-permute-start | bytes 2359304 | tf_op jit(solution)/shard_map/ppermute | solution.py:103
  262.7 15.1 %copy-start.6 = (f32[512,768]{1,0:T(8,128)S(1)}, f32[512,768]{1,0:T(8,128)}, u32[]{:S(2)}) copy-start(f32[512,768]{1,0:T(8,128)} %copy-done.5) | copy-start | bytes 4718596
  262.8 15.4 %collective-permute-start.35 = (bf16[512,768]{1,0:T(8,128)(2,1)S(1)}, bf16[512,768]{1,0:T(8,128)(2,1)S(1)}, u32[]{:S(2)}, u32[]{:S(2)}) collective-permute-start(bf16[512,768]{1,0:T(8,128)(2,1)S(1)} %add_convert_fusion), channel_id=1, source_target_pairs={{1,16},{3,18},{5,20},{7,22},{9,24},{11,26},{13,28},{15,30},{16,1},... | collective-permute-start | bytes 2359304 | tf_op jit(solution)/shard_map/ppermute | solution.py:103
  263.6 29.7 %collective-permute-start.33 = (bf16[512,768]{1,0:T(8,128)(2,1)}, bf16[512,768]{1,0:T(8,128)(2,1)S(1)}, u32[]{:S(2)}, u32[]{:S(2)}) collective-permute-start(bf16[512,768]{1,0:T(8,128)(2,1)} %add_convert_fusion.2), channel_id=1, source_target_pairs={{0,8},{2,10},{4,12},{6,14},{8,0},{10,2},{12,4},{14,6},{17,25},{19,... | collective-permute-start | bytes 2359304 | tf_op jit(solution)/shard_map/ppermute | solution.py:103
  297.1 4.4 %collective-permute-start.39 = (f32[256]{0:T(256)S(1)}, f32[256]{0:T(256)S(1)}, u32[]{:S(2)}, u32[]{:S(2)}) collective-permute-start(f32[256]{0:T(256)S(1)} %get-tuple-element.19), channel_id=1, source_target_pairs={{0,3},{1,0},{2,1},{3,2},{4,7},{5,4},{6,5},{7,6},{8,11},{9,8},{10,9... | collective-permute-start | bytes 3080 | tf_op jit(solution)/shard_map/ppermute | solution.py:103
  300.2 3.6 %collective-permute-start.40 = (f32[256]{0:T(256)S(1)}, f32[256]{0:T(256)S(1)}, u32[]{:S(2)}, u32[]{:S(2)}) collective-permute-start(f32[256]{0:T(256)S(1)} %get-tuple-element.18), channel_id=1, source_target_pairs={{0,2},{1,3},{2,0},{3,1},{4,6},{5,7},{6,4},{7,5},{8,10},{9,11},{10,... | collective-permute-start | bytes 3080 | tf_op jit(solution)/shard_map/ppermute | solution.py:103
  301.4 3.0 collective-permute-start.41
  304.5 3.7 %collective-permute-start.42 = (f32[4,8]{1,0:T(4,128)S(1)}, f32[4,8]{1,0:T(4,128)S(1)}, u32[]{:S(2)}, u32[]{:S(2)}) collective-permute-start(f32[4,8]{1,0:T(4,128)S(1)} %pad_maximum_fusion.6), channel_id=1, source_target_pairs={{0,4},{1,5},{2,6},{3,7},{4,0},{5,1},{6,2},{7,3},{8,12},{9,13},{10,... | collective-permute-start | bytes 392 | tf_op jit(solution)/shard_map/ppermute | solution.py:103
  308.2 8.2 %collective-permute-start.43 = (f32[4,8]{1,0:T(4,128)S(1)}, f32[4,8]{1,0:T(4,128)S(1)}, u32[]{:S(2)}, u32[]{:S(2)}) collective-permute-start(f32[4,8]{1,0:T(4,128)S(1)} %fusion.113), channel_id=1, source_target_pairs={{0,8},{1,9},{2,10},{3,11},{4,12},{5,13},{6,14},{7,15},{8,16},{9,17... | collective-permute-start | bytes 392 | tf_op jit(solution)/shard_map/ppermute | solution.py:103
  313.9 4.5 %collective-permute-start.44 = (f32[4,8]{1,0:T(4,128)S(1)}, f32[4,8]{1,0:T(4,128)S(1)}, u32[]{:S(2)}, u32[]{:S(2)}) collective-permute-start(f32[4,8]{1,0:T(4,128)S(1)} %fusion.113), channel_id=1, source_target_pairs={{0,16},{1,17},{2,18},{3,19},{4,20},{5,21},{6,22},{7,23},{8,24},{9,... | collective-permute-start | bytes 392 | tf_op jit(solution)/shard_map/ppermute | solution.py:103
  313.9 4.5 %collective-permute-start.45 = (f32[4,8]{1,0:T(4,128)S(1)}, f32[4,8]{1,0:T(4,128)S(1)}, u32[]{:S(2)}, u32[]{:S(2)}) collective-permute-start(f32[4,8]{1,0:T(4,128)S(1)} %fusion.113), channel_id=1, source_target_pairs={{0,24},{1,25},{2,26},{3,27},{4,28},{5,29},{6,30},{7,31},{8,0},{9,1... | collective-permute-start | bytes 392 | tf_op jit(solution)/shard_map/ppermute | solution.py:103
